TPU v7x, 256 devices: a whole 4x4x8 slice. The times are simulated.
256 devices in a mesh: bx: 8 (over z), by: 8 (over y, core), bz: 4 (over x).
Axes of the slice: x: 4, y: 4, z: 8, core: 2. Of those that a mesh axis runs over, the one named last changes fastest.
Arguments:
- positions: float32 [3, 1048576], P(None, ('bx', 'by', 'bz')), may hold values from -15 to 55, as said below
- velocities: float32 [3, 1048576], P(None, ('bx', 'by', 'bz')), may hold values from -6 to 6
- species: int32 [1048576], P(('bx', 'by', 'bz')), may hold values 0 or 1
- corner_slot: int32 [2, 8, 1048576], P(None, None, ('bx', 'by', 'bz')), may hold values from 0 to 255, as said below
- corner_weight: float32 [8, 1048576], P(None, ('bx', 'by', 'bz')), may hold values from 0 to 1, as said below
- slot_cell: int32 [3, 16384, 256], P(None, ('bx', 'by', 'bz')), may hold values from 0 to 63, as said below
- bond_pairs: int32 [2, 983040], P(None, ('bx', 'by', 'bz')), may hold values from 0 to 4095, as said below
Outputs:
- new_positions: float32 [3, 1048576], P(None, ('bx', 'by', 'bz'))
- new_velocities: float32 [3, 1048576], P(None, ('bx', 'by', 'bz'))
- smoothed: float32 [2, 128, 512, 256], P(None, 'bx', 'by', 'bz')
Inputs may be any that keep to these rules, and one draw needn't show every extreme that they name: `corner_slot`: row 0 is below 64 and row 1 below 256. For every owner and destination brick the named slots are those below a count of at least 32; the count is 256 for some destination of every owner, and for some brick of every z plane from all owners of that plane. `corner_weight`: for each bead the eight weights are the trilinear weights of a point inside a cell, corner c taking the upper side along x, y, z by bits 4, 2, 1 of c; they sum to one. `slot_cell`: row 0 is below 16, row 1 below 64, row 2 below 64. `bond_pairs`: bonds join beads of one device into chains of 16 beads; each bead lies in at most two bonds. `positions`: bonded beads stand at distance 1.
All inputs are finite; a program needn't handle non-finite values. No bound on the sum of `species` on one device may be relied on, other than what follows from the above.
Results may differ from a plain program's by a relative error of at most 0.0003.
Values sent between devices are 32-bit elements; how exact they have to be, the bound alone decides.
A program may use at most 128 MiB of HBM per device.

v0:
```python
import math

import jax
import jax.numpy as jnp
from jax import lax
from jax.sharding import Mesh
from jax.sharding import PartitionSpec as P

CX = 16
CY = 64
CZ = 64
BEADS_DEV = 4096
REACH = 3
SWEEPS = 4
BX_BY_BZ = ("bx", "by_0", "by_1", "bz")
BY = ("by_0", "by_1")
BX_BY = ("bx", "by_0", "by_1")


spread_cells = 1.0
mixing = 10.0
stiffness = 5.0
time_step = 0.1
bond_length = 1.0


def extended_2(cells, sides, width):
    for axis, dim in sides:
        count = lax.axis_size(axis)
        head = lax.slice_in_dim(cells, 0, width, axis=dim)
        tail = lax.slice_in_dim(cells, cells.shape[dim] - width, cells.shape[dim], axis=dim)
        cells = jnp.concatenate(
            [
                lax.ppermute(tail, axis, [(i, (i + 1) % count) for i in range(count)]),
                cells,
                lax.ppermute(head, axis, [((i + 1) % count, i) for i in range(count)]),
            ],
            axis=dim,
        )
    return cells


def cut_along(array, dim, count):
    lengths = array.shape
    pieces = array.reshape(*lengths[:dim], count, lengths[dim] // count, *lengths[dim + 1 :])
    return jnp.moveaxis(pieces, dim, 0)


def in_order(pieces, dim):
    pieces = jnp.moveaxis(pieces, 0, dim)
    lengths = pieces.shape
    return pieces.reshape(*lengths[:dim], lengths[dim] * lengths[dim + 1], *lengths[dim + 2 :])


def turned_blocks(pieces, axes, order):
    lengths = [lax.axis_size(a) for a in axes]
    pieces = pieces.reshape(*lengths, *pieces.shape[1:])
    for k in order:
        pieces = lax.all_to_all(pieces, axes[k], split_axis=k, concat_axis=k, tiled=True)
    return pieces.reshape(-1, *pieces.shape[len(axes) :])


def two_step_exchange(array, groups, order, split_dim, concat_dim):
    count = lax.axis_size(groups[0]) * lax.axis_size(groups[1])
    pieces = cut_along(array, split_dim, count)
    return in_order(turned_blocks(pieces, groups, order), concat_dim)


def gauss_taps():
    raw_list = [
        math.exp(-0.5 * (offset - REACH) ** 2 / spread_cells**2) for offset in range(2 * REACH + 1)
    ]
    tap_total = sum(raw_list)
    return [entry / tap_total for entry in raw_list]


def smooth_along(extended, axis):
    taps = gauss_taps()
    length = extended.shape[axis] - 2 * REACH
    result = jnp.zeros_like(lax.slice_in_dim(extended, 0, length, axis=axis))
    for offset in range(2 * REACH + 1):
        result = result + taps[offset] * lax.slice_in_dim(
            extended, offset, offset + length, axis=axis
        )
    return result


def smooth_brick(density, margin):
    width = REACH + margin
    extended = extended_2(density, (("bx", 1), (BY, 2), ("bz", 3)), width)
    return smooth_along(smooth_along(smooth_along(extended, 1), 2), 3)


def constrain(anchor, moved, first, second):
    separation = anchor[:, first] - anchor[:, second]
    for repeat in range(SWEEPS):
        stretch = moved[:, first] - moved[:, second]
        excess = jnp.sum(stretch * stretch, axis=0) - bond_length * bond_length
        intersection = jnp.maximum(
            jnp.sum(stretch * separation, axis=0), 0.5 * bond_length * bond_length
        )
        factor = excess / (4.0 * intersection)
        shifted = factor * separation
        moved = moved.at[:, first].add(-shifted).at[:, second].add(shifted)
    return moved


def on_device(positions, velocities, species, corner_slot, corner_weight, slot_cell, bond_pairs):
    plane = slot_cell.shape[1]
    slots = slot_cell.shape[2]
    cells = CX * CY * CZ
    is_lipid = (species == 0)[None, :]
    flat_slots = (corner_slot[0] * slots + corner_slot[1]).reshape(-1)
    both = jnp.stack(
        [jnp.where(is_lipid, corner_weight, 0.0), jnp.where(is_lipid, 0.0, corner_weight)]
    )
    packets = jnp.zeros((2, plane * slots), jnp.float32).at[:, flat_slots].add(both.reshape(2, -1))
    received = two_step_exchange(
        packets.reshape(2, plane, slots), (("bx", "by_0"), "by_1"), (1, 0), 1, 1
    )
    flat_cells = ((slot_cell[0] * CY + slot_cell[1]) * CZ + slot_cell[2]).reshape(-1)
    density = jnp.zeros((2, cells), jnp.float32).at[:, flat_cells].add(received.reshape(2, -1))
    density = density * (CX * CY * CZ / BEADS_DEV)
    density = density.reshape(2, CX, CY, CZ)
    margin = 1
    filtered = smooth_brick(density, margin)
    smoothed = filtered[:, margin : margin + CX, margin : margin + CY, margin : margin + CZ]
    combined = filtered[0] + filtered[1]
    potential = jnp.stack(
        [mixing * filtered[1] + stiffness * combined, mixing * filtered[0] + stiffness * combined]
    )
    slope_x = (potential[:, 2:, 1:-1, 1:-1] - potential[:, :-2, 1:-1, 1:-1]) * 0.5
    slope_y = (potential[:, 1:-1, 2:, 1:-1] - potential[:, 1:-1, :-2, 1:-1]) * 0.5
    slope_z = (potential[:, 1:-1, 1:-1, 2:] - potential[:, 1:-1, 1:-1, :-2]) * 0.5
    slopes = jnp.stack([slope_x, slope_y, slope_z], axis=1).reshape(6, cells)
    outgoing = slopes[:, flat_cells]
    returned = lax.all_to_all(
        outgoing.reshape(6, plane, slots), BX_BY, split_axis=1, concat_axis=1, tiled=True
    )
    table = returned.reshape(2, 3, plane * slots)
    count = corner_weight.shape[1]
    picked = jnp.where(
        is_lipid[None],
        table[0][:, flat_slots].reshape(3, 8, count),
        table[1][:, flat_slots].reshape(3, 8, count),
    )
    force = -jnp.sum(corner_weight[None] * picked, axis=1)
    half = velocities + 0.5 * time_step * force
    moved = positions + time_step * half
    moved = constrain(positions, moved, bond_pairs[0], bond_pairs[1])
    new_velocities = (moved - positions) / time_step
    return (moved, new_velocities, smoothed)


def solution(mesh):
    split = Mesh(
        mesh.devices.reshape(mesh.shape["bx"], 4, 2, mesh.shape["bz"]), ("bx", "by_0", "by_1", "bz")
    )
    placed = (
        P(None, BX_BY_BZ),
        P(None, BX_BY_BZ),
        P(BX_BY_BZ),
        P(None, None, BX_BY_BZ),
        P(None, BX_BY_BZ),
        P(None, BX_BY_BZ, None),
        P(None, BX_BY_BZ),
    )
    return jax.shard_map(
        on_device,
        mesh=split,
        in_specs=placed,
        out_specs=(P(None, BX_BY_BZ), P(None, BX_BY_BZ), P(None, "bx", BY, "bz")),
        check_vma=False,
    )
```

profile of v0, /device:TPU:1, one launch (start us, length us, event | category | flops | bytes accessed | tf_op | source)
XLA Modules:
  0.0 1106.0 jit_solution(18343486178446180231)
XLA Ops:
  2.8 8.3 copy.138
  11.5 177.9 %scatter_custom_fusion = f32[2,16384]{0,1:T(8,128)} fusion(s32[32768]{0:T(1024)S(1)} %bitcast.64, f32[32768,2]{1,0:T(8,128)} %copy.138, f32[]{:T(128)} %constant.20.clone.1), kind=kCustom, calls=%fused_computation.27 | custom fusion | flops 65536 | bytes 131584 | tf_op jit(solution)/shard_map/scatter-add | solution.py:117
  189.5 5.4 copy.139
  194.9 6.7 all_to_all.15
  202.3 9.5 all-to-all-start.1
  212.0 9.2 all-to-all-done.1
  221.2 4.8 copy.142
  226.0 101.0 %scatter_custom_fusion.1 = f32[2,65536]{0,1:T(8,128)} fusion(s32[16384]{0:T(1024)S(1)} %bitcast.69, f32[16384,2]{1,0:T(8,128)} %bitcast.61, f32[]{:T(128)} %constant.20.clone.1), kind=kCustom, calls=%fused_computation.25 | custom fusion | flops 32768 | bytes 524800 | tf_op jit(solution)/shard_map/scatter-add | solution.py:122
  327.0 22.3 %broadcast_multiply_fusion = f32[2,65536]{0,1:T(8,128)} fusion(f32[2,65536]{0,1:T(8,128)} %scatter_custom_fusion.1), kind=kLoop, calls=%fused_computation.24 | loop fusion | flops 131072 | bytes 1048576 | tf_op jit(solution)/shard_map/mul | solution.py:123
  349.3 18.1 %copy.143 = f32[2,16,64,64]{3,1,2,0:T(8,128)S(1)} copy(f32[2,16,64,64]{0,3,2,1:T(8,128)} %bitcast.54) | data formatting | bytes 1048576 | tf_op jit(solution)/shard_map/reshape | solution.py:124
  368.3 2.0 collective-permute-start.1
  370.9 3.7 collective-permute-done
  374.6 2.8 collective-permute-start.2
  377.7 1.4 collective-permute-done.2
  379.1 2.7 collective-permute-done.3
  382.7 1.8 fusion.66
  384.5 2.7 copy.146
  387.2 1.2 collective-permute-start.4
  388.4 1.2 copy.147
  389.7 1.5 collective-permute-start.5
  391.1 1.5 copy.158
  392.6 8.3 gather_fusion.5
  400.9 7.9 gather_fusion.6
  408.8 2.7 copy.148
  411.5 2.7 copy.149
  414.2 3.4 pad_maximum_fusion.2
  417.6 1.4 fusion.24
  419.5 2.6 fusion.30
  422.3 1.4 fusion.49
  425.0 2.3 reshape.218
  427.3 16.5 %copy.151 = f32[6,65536]{0,1:T(8,128)} copy(f32[6,65536]{1,0:T(8,128)} %reshape.218) | data formatting | bytes 3145728 | tf_op jit(solution)/shard_map/reshape | solution.py:135
  443.8 64.9 %gather_fusion = f32[16384,6]{1,0:T(8,128)} fusion(f32[6,65536]{0,1:T(8,128)} %copy.151, s32[16384]{0:T(1024)S(1)} %copy-done.10), kind=kCustom, calls=%fused_computation | custom fusion | bytes 851968 | tf_op jit(solution)/shard_map/gather | solution.py:136
  508.7 6.1 copy.152
  514.8 8.4 all-to-all-start.2
  523.7 1.3 copy.164
  524.9 16.0 %all-to-all-done.2 = f32[6,64,256]{2,0,1:T(8,128)S(1)} async-done(((f32[6,64,256]{2,0,1:T(8,128)}), f32[6,64,256]{2,0,1:T(8,128)S(1)}, u32[]{:S(2)}, u32[]{:S(2)}) %all-to-all-start.2) | async-done | bytes 393248 | tf_op jit(solution)/shard_map/all_to_all | solution.py:137
  541.1 4.8 copy.154
  545.9 4.8 copy.153
  550.7 111.6 %gather_fusion.2 = f32[32768,3]{1,0:T(8,128)} fusion(f32[3,16384]{0,1:T(8,128)} %bitcast.56, s32[32768]{0:T(1024)S(1)} %broadcast_clamp_fusion), kind=kCustom, calls=%fused_computation.2 | custom fusion | bytes 917504 | tf_op jit(solution)/shard_map/gather | solution.py:145
  662.3 111.6 %gather_fusion.1 = f32[32768,3]{1,0:T(8,128)} fusion(f32[3,16384]{0,1:T(8,128)} %bitcast.57, s32[32768]{0:T(1024)S(1)} %broadcast_clamp_fusion), kind=kCustom, calls=%fused_computation.1 | custom fusion | bytes 917504 | tf_op jit(solution)/shard_map/gather | solution.py:144
  773.9 14.3 %multiply_reduce_fusion = f32[3,4096]{0,1:T(8,128)S(1)} fusion(f32[3,8,4096]{0,2,1:T(8,128)} %bitcast.59, f32[3,8,4096]{0,2,1:T(8,128)} %bitcast.58, f32[8,4096]{1,0:T(8,128)S(1)} %copy-done.6, pred[4096]{0:T(1024)(128)(4,1)S(1)} %copy-done.17), kind=kLoop, calls=%fused_computation.23 | loop fusion | flops 282624 | bytes 970752 | tf_op jit(solution)/shard_map/reduce_sum | solution.py:147
  789.8 7.9 gather_fusion.4
  797.7 7.9 gather_fusion.3
  805.6 4.4 multiply_reduce_fusion.8
  810.0 27.6 %scatter_custom_fusion.2 = f32[3,4096]{0,1:T(8,128)} fusion(f32[3,4096]{0,1:T(8,128)} %copy-done, s32[3840]{0:T(1024)} %copy-done.15, f32[3840,3]{1,0:T(8,128)S(1)} %get-tuple-element.34, f32[3840]{0:T(1024)S(1)} %multiply_divide_fusion.3), kind=kCustom, calls=%fused_computation.47 | custom fusion | flops 34560 | bytes 110592 | tf_op jit(solution)/shard_map/scatter-add | solution.py:104
  837.6 27.7 %scatter_custom_fusion.3 = f32[3,4096]{0,1:T(8,128)} fusion(f32[3,4096]{0,1:T(8,128)} %scatter_custom_fusion.2, s32[3840]{0:T(1024)S(1)} %get-tuple-element.32, f32[3840,3]{1,0:T(8,128)S(1)} %get-tuple-element.34, f32[3840]{0:T(1024)S(1)} %multiply_divide_fusion.3), kind=kCustom, calls=%fused_computation.66 | custom fusion | flops 23040 | bytes 2031616 | tf_op jit(solution)/shard_map/scatter-add | solution.py:104
  865.3 9.5 gather_fusion.8
  874.8 9.4 gather_fusion.7
  884.3 3.2 multiply_reduce_fusion.6
  887.5 27.6 %scatter_custom_fusion.4 = f32[3,4096]{0,1:T(8,128)} fusion(f32[3,4096]{0,1:T(8,128)} %scatter_custom_fusion.3, s32[3840]{0:T(1024)} %copy-done.15, f32[3840,3]{1,0:T(8,128)S(1)} %get-tuple-element.34, f32[3840]{0:T(1024)S(1)} %multiply_divide_fusion.2), kind=kCustom, calls=%fused_computation.45 | custom fusion | flops 34560 | bytes 110592 | tf_op jit(solution)/shard_map/scatter-add | solution.py:104
  915.2 27.5 %scatter_custom_fusion.5 = f32[3,4096]{0,1:T(8,128)} fusion(f32[3,4096]{0,1:T(8,128)} %scatter_custom_fusion.4, s32[3840]{0:T(1024)S(1)} %get-tuple-element.32, f32[3840,3]{1,0:T(8,128)S(1)} %get-tuple-element.34, f32[3840]{0:T(1024)S(1)} %multiply_divide_fusion.2), kind=kCustom, calls=%fused_computation.63 | custom fusion | flops 23040 | bytes 2031616 | tf_op jit(solution)/shard_map/scatter-add | solution.py:104
  942.7 9.5 gather_fusion.10
  952.1 9.4 gather_fusion.9
  961.6 3.2 multiply_reduce_fusion.4
  964.8 27.9 %scatter_custom_fusion.6 = f32[3,4096]{0,1:T(8,128)} fusion(f32[3,4096]{0,1:T(8,128)} %scatter_custom_fusion.5, s32[3840]{0:T(1024)} %copy-done.15, f32[3840,3]{1,0:T(8,128)S(1)} %get-tuple-element.34, f32[3840]{0:T(1024)S(1)} %multiply_divide_fusion.1), kind=kCustom, calls=%fused_computation.43 | custom fusion | flops 34560 | bytes 110592 | tf_op jit(solution)/shard_map/scatter-add | solution.py:104
  992.7 27.5 %scatter_custom_fusion.7 = f32[3,4096]{0,1:T(8,128)} fusion(f32[3,4096]{0,1:T(8,128)} %scatter_custom_fusion.6, s32[3840]{0:T(1024)S(1)} %get-tuple-element.32, f32[3840,3]{1,0:T(8,128)S(1)} %get-tuple-element.34, f32[3840]{0:T(1024)S(1)} %multiply_divide_fusion.1), kind=kCustom, calls=%fused_computation.60 | custom fusion | flops 23040 | bytes 2031616 | tf_op jit(solution)/shard_map/scatter-add | solution.py:104
  1020.2 9.5 gather_fusion.12
  1029.7 9.4 gather_fusion.11
  1039.2 3.2 multiply_reduce_fusion.2
  1042.4 27.6 %scatter_custom_fusion.8 = f32[3,4096]{0,1:T(8,128)} fusion(f32[3,4096]{0,1:T(8,128)} %scatter_custom_fusion.7, s32[3840]{0:T(1024)} %copy-done.15, f32[3840,3]{1,0:T(8,128)S(1)} %get-tuple-element.34, f32[3840]{0:T(1024)S(1)} %multiply_divide_fusion), kind=kCustom, calls=%fused_computation.41 | custom fusion | flops 34560 | bytes 110592 | tf_op jit(solution)/shard_map/scatter-add | solution.py:104
  1070.1 27.5 %scatter_custom_fusion.9 = f32[3,4096]{0,1:T(8,128)} fusion(f32[3,4096]{0,1:T(8,128)} %scatter_custom_fusion.8, s32[3840]{0:T(1024)S(1)} %get-tuple-element.32, f32[3840,3]{1,0:T(8,128)S(1)} %get-tuple-element.34, f32[3840]{0:T(1024)S(1)} %multiply_divide_fusion), kind=kCustom, calls=%fused_computation.57 | custom fusion | flops 23040 | bytes 2031616 | tf_op jit(solution)/shard_map/scatter-add | solution.py:104
  1097.6 3.9 subtract_multiply_fusion
  1101.4 1.2 copy.162
  1102.7 2.8 copy.163
  (76 shorter events, 10.3 us)
Async XLA Ops:
  1.4 1.2 copy-start.16
  2.8 8.4 copy-start.11
  11.5 178.0 %copy-start.7 = (s32[32768,1]{0,1:T(1,128)}, s32[32768,1]{0,1:T(1,128)S(1)}, u32[]{:S(2)}) copy-start(s32[32768,1]{0,1:T(1,128)S(1)} %compare_select_fusion) | copy-start | bytes 393220
  189.5 22.4 %copy-start.13 = (s32[3,64,256]{2,1,0:T(8,128)S(1)}, s32[3,64,256]{2,1,0:T(8,128)}, u32[]{:S(2)}) copy-start(s32[3,64,256]{2,1,0:T(8,128)} %param.12) | copy-start | bytes 589828
  202.3 18.9 %all-to-all-start.1 = ((f32[32,2,2,1,256]{4,2,3,1,0:T(2,128)}), f32[32,2,2,1,256]{4,2,3,1,0:T(2,128)S(1)}, u32[]{:S(2)}, u32[]{:S(2)}) async-start(f32[32,2,2,1,256]{4,2,3,1,0:T(2,128)} %copy.141), calls=%async_computation.1 | async-start | bytes 262144 | tf_op jit(solution)/shard_map/all_to_all | solution.py:59
  367.4 10.2 copy-start.18
  367.5 7.1 collective-permute-start
  368.3 6.3 collective-permute-start.1
  374.6 7.2 copy-start.5
  374.6 4.5 collective-permute-start.2
  377.4 4.3 collective-permute-start.3
  377.7 13.4 %copy-start.15 = (s32[3840]{0:T(1024)}, s32[3840]{0:T(1024)S(1)}, u32[]{:S(2)}) copy-start(s32[3840]{0:T(1024)S(1)} %get-tuple-element.33) | copy-start | bytes 46084
  381.8 0.6 copy-start.9
  387.2 21.6 %collective-permute-start.4 = (f32[2,24,72,4]{2,1,3,0:T(8,128)}, f32[2,24,72,4]{2,1,3,0:T(8,128)}, u32[]{:S(2)}, u32[]{:S(2)}) collective-permute-start(f32[2,24,72,4]{2,1,3,0:T(8,128)} %copy.146), channel_id=1, source_target_pairs={{0,1},{1,2},{2,3},{3,0},{4,5},{5,6},{6,7},{7,4},{8,9},{9,10},{10,1... | collective-permute-start | bytes 165896 | tf_op jit(solution)/shard_map/ppermute | solution.py:34
  389.7 21.8 %collective-permute-start.5 = (f32[2,24,72,4]{2,1,3,0:T(8,128)}, f32[2,24,72,4]{2,1,3,0:T(8,128)}, u32[]{:S(2)}, u32[]{:S(2)}) collective-permute-start(f32[2,24,72,4]{2,1,3,0:T(8,128)} %copy.147), channel_id=1, source_target_pairs={{1,0},{2,1},{3,2},{0,3},{5,4},{6,5},{7,6},{4,7},{9,8},{10,9},{11,1... | collective-permute-start | bytes 165896 | tf_op jit(solution)/shard_map/ppermute | solution.py:36
  392.6 21.6 %copy-start.2 = (f32[3,4096]{0,1:T(8,128)}, f32[3,4096]{0,1:T(8,128)S(1)}, u32[]{:S(2)}) copy-start(f32[3,4096]{0,1:T(8,128)S(1)} %copy.158) | copy-start | bytes 147460
  422.1 1.6 copy-start.3
  427.3 16.5 %copy-start.10 = (s32[16384]{0:T(1024)S(1)}, s32[16384]{0:T(1024)}, u32[]{:S(2)}) copy-start(s32[16384]{0:T(1024)} %broadcast_clamp_fusion.1) | copy-start | bytes 196612
  508.7 14.5 %copy-start.8 = (s32[32768,1]{0,1:T(1,128)S(1)}, s32[32768,1]{0,1:T(1,128)}, u32[]{:S(2)}) copy-start(s32[32768,1]{0,1:T(1,128)} %copy-done.7) | copy-start | bytes 393220
  508.7 14.6 %copy-start.4 = (f32[2,18,66,66]{3,1,2,0:T(8,128)S(1)}, f32[2,18,66,66]{3,1,2,0:T(8,128)}, u32[]{:S(2)}) copy-start(f32[2,18,66,66]{3,1,2,0:T(8,128)} %copy-done.3) | copy-start | bytes 1881796
  514.8 26.1 %all-to-all-start.2 = ((f32[6,64,256]{2,0,1:T(8,128)}), f32[6,64,256]{2,0,1:T(8,128)S(1)}, u32[]{:S(2)}, u32[]{:S(2)}) async-start(f32[6,64,256]{2,0,1:T(8,128)} %copy.152), calls=%async_computation.2 | async-start | bytes 1048576 | tf_op jit(solution)/shard_map/all_to_all | solution.py:137
  662.3 111.6 %copy-start.6 = (f32[8,4096]{1,0:T(8,128)S(1)}, f32[8,4096]{1,0:T(8,128)}, u32[]{:S(2)}) copy-start(f32[8,4096]{1,0:T(8,128)} %param.11) | copy-start | bytes 393220
  662.3 111.6 %copy-start.17 = (pred[4096]{0:T(1024)(128)(4,1)S(1)}, pred[4096]{0:T(1024)(128)(4,1)}, u32[]{:S(2)}) copy-start(pred[4096]{0:T(1024)(128)(4,1)} %copy-done.16) | copy-start | bytes 12292
  788.2 0.8 copy-start.12
  788.2 0.9 copy-start.14
  789.8 7.9 copy-start
  1097.5 3.9 copy-start.1
where the time goes:
time: 1120 us; the launch traced here: 1110 us
  other arithmetic  568 us (51%)
  local copies, waits for them, and re-layouts  471 us (42%)
  waiting for transfers between devices  32.9 us (3%)
  starting transfers between devices  26.3 us (2%)
    scatter-add x8, other arithmetic, constrain(): moved = moved.at[:, first].add(-shifted).at[:, second].add(shifted)  221 us
    scatter-add x1, other arithmetic, on_device(): jnp.zeros((2, plane * slots), jnp.float32).at[:, flat_slots]  178 us
    gather x1, local copies, waits for them, and re-layouts, on_device(): table[0][:, flat_slots].reshape(3, 8, count)  112 us
    gather x1, local copies, waits for them, and re-layouts, on_device(): table[1][:, flat_slots].reshape(3, 8, count)  112 us
    scatter-add x1, other arithmetic, on_device(): jnp.zeros((2, cells), jnp.float32).at[:, flat_cells]  101 us
    gather x8, local copies, waits for them, and re-layouts, constrain(): stretch = moved[:, first] - moved[:, second]  72.6 us
    gather x1, local copies, waits for them, and re-layouts, on_device(): outgoing = slopes[:, flat_cells]  64.9 us
  transfers between devices with their start and end apart: 8, of which 5 were waited for; matrix products, arithmetic and copies ran while one was open for 2% of the time, Pallas kernels for 0%

commit v1 on v0

v1 whole, which is shorter than its diff:
```python
import functools
import math

import jax
import jax.numpy as jnp
import numpy as np
from jax import lax
from jax.experimental import pallas as pl
from jax.experimental.pallas import tpu as pltpu
from jax.sharding import PartitionSpec as P

CX = 16
CY = 64
CZ = 64
BEADS_DEV = 4096
REACH = 3
SWEEPS = 4
SLOTS = 256
PLANE = 64
BONDS_DEV = 3840
OWNERS = ("bx", "by", "bz")
PLANE_AXES = ("bx", "by")

spread_cells = 1.0
mixing = 10.0
stiffness = 5.0
time_step = 0.1

F32 = jnp.float32
BF16 = jnp.bfloat16
NT = (((1,), (1,)), ((), ()))
NN = (((1,), (0,)), ((), ()))


def gauss_taps():
    raw_list = [
        math.exp(-0.5 * (offset - REACH) ** 2 / spread_cells**2) for offset in range(2 * REACH + 1)
    ]
    tap_total = sum(raw_list)
    return [entry / tap_total for entry in raw_list]


def mm(a, b, dims=NN):
    return lax.dot_general(a, b, dims, preferred_element_type=F32)


def two(x):
    hi = x.astype(BF16)
    return hi, (x - hi.astype(F32)).astype(BF16)


def three(x):
    hi = x.astype(BF16)
    rest = x - hi.astype(F32)
    mid = rest.astype(BF16)
    return hi, mid, (rest - mid.astype(F32)).astype(BF16)


def rows_iota(rows, n, dtype=BF16):
    return lax.broadcasted_iota(jnp.int32, (rows, n), 0).astype(F32).astype(dtype)


def onehot(index, rows):
    return jnp.where(
        rows_iota(rows, index.shape[1]) == index.astype(F32).astype(BF16),
        jnp.ones((), BF16),
        jnp.zeros((), BF16),
    )


def weighted(index, rows, value):
    return jnp.where(
        rows_iota(rows, index.shape[1]) == index.astype(F32).astype(BF16),
        value,
        jnp.zeros((), BF16),
    )


def pick(index, rows, values):
    n = index.shape[1]
    mask = lax.broadcasted_iota(jnp.int32, (rows, n), 0) == index
    return [
        jnp.sum(jnp.where(mask, values[g * rows : (g + 1) * rows], 0.0), axis=0, keepdims=True)
        for g in range(values.shape[0] // rows)
    ]


PACK_CHUNK = 1024


def pack_kernel(slot_ref, weight_ref, species_ref, out_ref, acc_ref):
    acc_ref[...] = jnp.zeros_like(acc_ref)

    def body(step, carry):
        c = step % 8
        cols = pl.ds(pl.multiple_of((step // 8) * PACK_CHUNK, PACK_CHUNK), PACK_CHUNK)
        brick = slot_ref[0, pl.ds(c, 1), cols]
        slot = slot_ref[1, pl.ds(c, 1), cols]
        kd = brick + PLANE * species_ref[:, cols]
        hi, lo = two(weight_ref[pl.ds(c, 1), cols])
        left = jnp.concatenate([weighted(kd, 2 * PLANE, hi), weighted(kd, 2 * PLANE, lo)], axis=0)
        acc_ref[...] += mm(left, onehot(slot, SLOTS), NT)
        return carry

    lax.fori_loop(0, 8 * BEADS_DEV // PACK_CHUNK, body, 0)
    total = acc_ref[: 2 * PLANE] + acc_ref[2 * PLANE :]
    out_ref[:, :SLOTS] = total[:PLANE]
    out_ref[:, SLOTS:] = total[PLANE:]


SPREAD_ROWS = 8


def onehot_xy(x, y):
    oy = onehot(y, CY)
    xb = x.astype(F32).astype(BF16)
    zero = jnp.zeros((), BF16)
    blocks = []
    for i in range(CX):
        blocks.append(jnp.where(xb == jnp.asarray(i, BF16), oy, zero))
    return jnp.concatenate(blocks, axis=0)


def spread_kernel(recv_ref, cell_ref, out_ref, xy_ref, z_ref, acc_ref):
    acc_ref[...] = jnp.zeros_like(acc_ref)

    def body(step, carry):
        for i in range(SPREAD_ROWS):
            p = step * SPREAD_ROWS + i
            x, y, z = (cell_ref[a, pl.ds(p, 1), :] for a in range(3))
            cols = slice(i * SLOTS, (i + 1) * SLOTS)
            xy_ref[:, cols] = onehot_xy(x, y)
            for k in range(2):
                hi, lo = two(recv_ref[pl.ds(p, 1), k * SLOTS : (k + 1) * SLOTS])
                z_ref[k * CZ : (k + 1) * CZ, cols] = weighted(z, CZ, hi)
                z_ref[(2 + k) * CZ : (3 + k) * CZ, cols] = weighted(z, CZ, lo)
        acc_ref[...] += mm(xy_ref[...], z_ref[...], NT)
        return carry

    lax.fori_loop(0, PLANE // SPREAD_ROWS, body, 0)
    total = (acc_ref[:, : 2 * CZ] + acc_ref[:, 2 * CZ :]) * (CX * CY * CZ / BEADS_DEV)
    out_ref[...] = total.reshape(CX, CY, 2 * CZ)


def filter_x_kernel(left_ref, own_ref, right_ref, out_ref, head_ref, tail_ref, ext_ref):
    taps = gauss_taps()
    w = REACH + 1
    ext_ref[:w] = left_ref[...]
    ext_ref[w : w + CX] = own_ref[...]
    ext_ref[w + CX :] = right_ref[...]

    def body(i, carry):
        total = taps[0] * ext_ref[i]
        for j in range(1, 2 * REACH + 1):
            total = total + taps[j] * ext_ref[i + j]
        out_ref[i] = total
        head_ref[i] = total[:w]
        tail_ref[i] = total[CY - w :]
        return carry

    lax.fori_loop(0, CX + 2, body, 0)


YP = 72


def filter_y_kernel(left_ref, own_ref, right_ref, out_ref, edge_ref, ext_ref):
    taps = gauss_taps()
    w = REACH + 1
    span = CY + 2
    ext_ref[:, :w] = left_ref[...]
    ext_ref[:, w : w + CY] = own_ref[...]
    ext_ref[:, w + CY :] = right_ref[...]
    row = lax.broadcasted_iota(jnp.int32, (16, 2 * CZ), 0)
    lane = lax.broadcasted_iota(jnp.int32, (16, 2 * CZ), 1)
    wanted = ((row % 8) // w) * CZ + (row // 8) * (CZ - w) + row % w
    select = jnp.where(lane == wanted, 1.0, 0.0).astype(BF16)

    def body(i, carry):
        total = taps[0] * ext_ref[i, :span]
        for j in range(1, 2 * REACH + 1):
            total = total + taps[j] * ext_ref[i, j : j + span]
        full = jnp.concatenate([total, jnp.zeros((YP - span, 2 * CZ), F32)], axis=0)
        out_ref[i] = full
        hi, mid, lo = three(full)
        edge_ref[i] = mm(select, hi, NT) + mm(select, mid, NT) + mm(select, lo, NT)
        return carry

    lax.fori_loop(0, CX + 2, body, 0)


def z_operators():
    taps = gauss_taps()
    w = REACH + 1
    smooth = np.zeros((CZ + 2 * w, CZ))
    slope = np.zeros((CZ + 2 * w, CZ))
    for z in range(CZ):
        for j in range(2 * REACH + 1):
            smooth[z + w + j - REACH, z] += taps[j]
            slope[z + w + 1 + j - REACH, z] += 0.5 * taps[j]
            slope[z + w - 1 + j - REACH, z] -= 0.5 * taps[j]
    mix = np.array([[stiffness, mixing + stiffness], [mixing + stiffness, stiffness]])
    full = np.concatenate(
        [np.kron(np.eye(2), smooth), np.kron(mix.T, smooth), np.kron(mix.T, slope)], axis=1
    ).reshape(2, CZ + 2 * w, 6 * CZ)
    own = full[:, w : w + CZ].reshape(2 * CZ, 6 * CZ)
    halo = np.concatenate(
        [full[:, :w].reshape(2 * w, 6 * CZ), full[:, w + CZ :].reshape(2 * w, 6 * CZ)]
    )
    return own.astype(np.float32), halo.astype(np.float32)


def mm3(a, b_hi, b_lo):
    a_hi, a_lo = two(a)
    return mm(a_hi, b_hi) + (mm(a_hi, b_lo) + mm(a_lo, b_hi))


GATHER_ROWS = 2


def slopes_kernel(
    own_ref, left_ref, right_ref, op_ref, hop_ref, smooth_ref, table_ref, p_ref, pz_ref
):
    op_hi, op_lo = two(op_ref[...])
    hop_hi, hop_lo = two(hop_ref[...])
    wide = 2 * CZ

    def filter_z(i, carry):
        halo = jnp.concatenate([left_ref[i], right_ref[i]], axis=0).T
        both = mm3(own_ref[i], op_hi, op_lo) + mm3(halo, hop_hi, hop_lo)
        p_ref[i] = both[:, wide : 2 * wide]
        pz_ref[i] = both[:, 2 * wide :]

        @pl.when((i > 0) & (i <= CX))
        def _():
            for k in range(2):
                smooth_ref[k, i - 1] = both[1 : CY + 1, k * CZ : (k + 1) * CZ]

        return carry

    lax.fori_loop(0, CX + 2, filter_z, 0)

    for i in range(0, CX, 2):
        parts = []
        for q in (i + 1, i + 2):
            sx = (p_ref[q + 1, 1 : CY + 1] - p_ref[q - 1, 1 : CY + 1]) * 0.5
            sy = (p_ref[q, 2 : CY + 2] - p_ref[q, :CY]) * 0.5
            sz = pz_ref[q, 1 : CY + 1]
            parts.append((sx, sy, sz))
        cols = slice(i * CY, (i + 2) * CY)
        for a in range(3):
            hi, lo = two(jnp.concatenate([parts[0][a], parts[1][a]], axis=0).T)
            table_ref[a * wide : (a + 1) * wide, cols] = hi
            table_ref[(3 + a) * wide : (4 + a) * wide, cols] = lo


def lookup_kernel(table_ref, cell_ref, out_ref):
    def body(step, carry):
        p0 = step * GATHER_ROWS
        xyz = [
            jnp.concatenate(
                [cell_ref[a, pl.ds(p0 + i, 1), :] for i in range(GATHER_ROWS)], axis=1
            )
            for a in range(3)
        ]
        both = mm(table_ref[...], onehot_xy(xyz[0], xyz[1]))
        half = 6 * CZ
        found = pick(xyz[2], CZ, both[:half] + both[half:])
        for g in range(6):
            for i in range(GATHER_ROWS):
                out_ref[g, pl.ds(p0 + i, 1), :] = found[g][:, i * SLOTS : (i + 1) * SLOTS]
        return carry

    lax.fori_loop(0, PLANE // GATHER_ROWS, body, 0)


HALF = BONDS_DEV
ENDS = 2 * BONDS_DEV


def to_rows(x):
    return jnp.concatenate([x[:, i : i + 128] for i in range(0, x.shape[1], 128)], axis=0)


def to_line(x):
    return jnp.concatenate([x[i : i + 1] for i in range(x.shape[0])], axis=1)


def bonds_kernel(pairs_ref, positions_ref, out_ref, oh_ref):
    pairs = jnp.concatenate([pairs_ref[0:1], pairs_ref[1:2]], axis=1)
    hi_index = pairs >> 7
    oh_ref[...] = onehot(pairs & 127, 128)
    number = lax.broadcasted_iota(jnp.int32, (1, HALF), 1)
    number = jnp.concatenate([number, number], axis=1)
    sign = jnp.where(lax.broadcasted_iota(jnp.int32, (1, ENDS), 1) < HALF, 1.0, -1.0)
    left = jnp.concatenate(
        [
            weighted(hi_index, 32, v.astype(F32).astype(BF16))
            for v in (number >> 6, number & 63, sign)
        ],
        axis=0,
    )
    sums = mm(left, oh_ref[...], NT).astype(BF16)
    high, low, signs = pick(hi_index, 32, mm(sums, oh_ref[...]))
    other = 64.0 * high + low - number.astype(F32)
    other_sign = signs - sign
    parts = [three(to_rows(positions_ref[a : a + 1])) for a in range(3)]
    table = [jnp.concatenate([parts[a][q] for a in range(3)], axis=0) for q in range(3)]
    oh = oh_ref[...]
    ends = pick(hi_index, 32, mm(table[0], oh) + mm(table[1], oh) + mm(table[2], oh))
    for a in range(3):
        out_ref[a : a + 1] = ends[a][:, :HALF] - ends[a][:, HALF:]
    out_ref[3:4] = other[:, :HALF]
    out_ref[4:5] = other[:, HALF:]
    out_ref[5:6] = other_sign[:, :HALF]
    out_ref[6:7] = other_sign[:, HALF:]
    out_ref[7:8] = jnp.zeros((1, HALF), F32)


FORCE_CHUNK = 512


def force_kernel(
    table_ref, slot_ref, weight_ref, species_ref, pos_ref, vel_ref, delta_ref, hi_ref, lo_ref
):
    hi, lo = two(table_ref[...])
    hi_ref[...] = hi
    lo_ref[...] = lo
    wide = 2 * PLANE

    def body(step, carry):
        cols = pl.ds(pl.multiple_of(step * FORCE_CHUNK, FORCE_CHUNK), FORCE_CHUNK)
        species = species_ref[:, cols]
        force = [jnp.zeros((1, FORCE_CHUNK), F32)] * 3
        for c in range(8):
            oh = onehot(slot_ref[1, c : c + 1, cols], SLOTS)
            both = mm(hi_ref[...], oh) + mm(lo_ref[...], oh)
            found = pick(slot_ref[0, c : c + 1, cols] + PLANE * species, wide, both)
            weight = weight_ref[c : c + 1, cols]
            force = [force[a] - weight * found[a] for a in range(3)]
        for a in range(3):
            half = vel_ref[a : a + 1, cols] + 0.5 * time_step * force[a]
            delta_ref[a : a + 1, cols] = time_step * half
        return carry

    lax.fori_loop(0, BEADS_DEV // FORCE_CHUNK, body, 0)


def constrain_kernel(pairs_ref, bonds_ref, delta_ref, pos_ref, newpos_ref, newvel_ref, oh_ref, nb_ref):
    pairs = jnp.concatenate([pairs_ref[0:1], pairs_ref[1:2]], axis=1)
    hi_index = pairs >> 7
    oh_ref[...] = onehot(pairs & 127, 128)
    r = [bonds_ref[a : a + 1] for a in range(3)]
    other = jnp.concatenate([bonds_ref[3:4], bonds_ref[4:5]], axis=1).astype(jnp.int32)
    sign = [bonds_ref[5:6], bonds_ref[6:7]]
    other_hi = other >> 7
    nb_ref[...] = onehot(other & 127, 128)
    delta = [delta_ref[a : a + 1] for a in range(3)]
    parts = [two(to_rows(d)) for d in delta]
    table = [jnp.concatenate([parts[a][q] for a in range(3)], axis=0) for q in range(2)]
    ends = pick(hi_index, 32, mm(table[0], oh_ref[...]) + mm(table[1], oh_ref[...]))
    v = [r[a] + (ends[a][:, :HALF] - ends[a][:, HALF:]) for a in range(3)]
    total = [jnp.zeros((1, HALF), F32)] * 3
    for sweep in range(SWEEPS):
        vv = v[0] * v[0] + v[1] * v[1] + v[2] * v[2]
        vr = v[0] * r[0] + v[1] * r[1] + v[2] * r[2]
        g = (vv - 1.0) / (4.0 * jnp.maximum(vr, 0.5))
        shift = [g * r[a] for a in range(3)]
        total = [total[a] + shift[a] for a in range(3)]
        if sweep + 1 == SWEEPS:
            break
        pad = jnp.zeros((2, 128), F32)
        parts = [two(jnp.concatenate([to_rows(s), pad], axis=0)) for s in shift]
        table = [jnp.concatenate([parts[a][q] for a in range(3)], axis=0) for q in range(2)]
        near = pick(other_hi, 32, mm(table[0], nb_ref[...]) + mm(table[1], nb_ref[...]))
        v = [
            v[a] - 2.0 * shift[a] - sign[0] * near[a][:, :HALF] + sign[1] * near[a][:, HALF:]
            for a in range(3)
        ]
    rows = []
    for a in range(3):
        both = jnp.concatenate([total[a], -total[a]], axis=1)
        rows += [weighted(hi_index, 32, q) for q in two(both)]
    moved = mm(jnp.concatenate(rows, axis=0), oh_ref[...], NT)
    for a in range(3):
        q = to_line(moved[64 * a : 64 * a + 32] + moved[64 * a + 32 : 64 * a + 64])
        change = delta[a] - q
        newpos_ref[a : a + 1] = pos_ref[a : a + 1] + change
        newvel_ref[a : a + 1] = change / time_step


def call(kernel, out_shapes, scratch, name):
    many = isinstance(out_shapes, list)
    shapes = [jax.ShapeDtypeStruct(s, d) for s, d in (out_shapes if many else [out_shapes])]
    return pl.pallas_call(
        kernel,
        out_shape=shapes if many else shapes[0],
        scratch_shapes=scratch,
        compiler_params=pltpu.CompilerParams(vmem_limit_bytes=60 * 1024 * 1024),
        name=name,
    )


def neighbours(head, tail, axis):
    count = lax.axis_size(axis)
    up = [(i, (i + 1) % count) for i in range(count)]
    down = [((i + 1) % count, i) for i in range(count)]
    return lax.ppermute(tail, axis, up), lax.ppermute(head, axis, down)


def on_device(positions, velocities, species, corner_slot, corner_weight, slot_cell, bond_pairs):
    w = REACH + 1
    wide = 2 * CZ
    species = species[None, :]
    packets = call(pack_kernel, ((PLANE, 2 * SLOTS), F32), [pltpu.VMEM((256, SLOTS), F32)], "pack")(
        corner_slot, corner_weight, species
    )
    bonds = call(
        bonds_kernel, ((8, BONDS_DEV), F32), [pltpu.VMEM((128, ENDS), BF16)], "bonds"
    )(bond_pairs, positions)
    received = lax.all_to_all(packets, PLANE_AXES, split_axis=0, concat_axis=0, tiled=True)
    density = call(
        spread_kernel,
        ((CX, CY, wide), F32),
        [
            pltpu.VMEM((CX * CY, SPREAD_ROWS * SLOTS), BF16),
            pltpu.VMEM((4 * CZ, SPREAD_ROWS * SLOTS), BF16),
            pltpu.VMEM((CX * CY, 4 * CZ), F32),
        ],
        "spread",
    )(received, slot_cell)
    left, right = neighbours(density[:w], density[CX - w :], "bx")
    along_x, head, tail = call(
        filter_x_kernel,
        [((CX + 2, CY, wide), F32), ((CX + 2, w, wide), F32), ((CX + 2, w, wide), F32)],
        [pltpu.VMEM((CX + 2 * w, CY, wide), F32)],
        "filter_x",
    )(left, density, right)
    left, right = neighbours(head, tail, "by")
    along_y, edge = call(
        filter_y_kernel,
        [((CX + 2, YP, wide), F32), ((CX + 2, 16, YP), F32)],
        [pltpu.VMEM((CX + 2, CY + 2 * w, wide), F32)],
        "filter_y",
    )(left, along_x, right)
    left, right = neighbours(edge[:, :8], edge[:, 8:], "bz")
    own_op, halo_op = z_operators()
    smoothed, table = call(
        slopes_kernel,
        [((2, CX, CY, CZ), F32), ((6 * wide, CX * CY), BF16)],
        [pltpu.VMEM((CX + 2, YP, wide), F32), pltpu.VMEM((CX + 2, YP, wide), F32)],
        "slopes",
    )(along_y, left, right, jnp.asarray(own_op), jnp.asarray(halo_op))
    outgoing = call(lookup_kernel, ((6, PLANE, SLOTS), F32), [], "lookup")(table, slot_cell)
    returned = lax.all_to_all(outgoing, PLANE_AXES, split_axis=1, concat_axis=1, tiled=True)
    delta = call(
        force_kernel,
        ((3, BEADS_DEV), F32),
        [pltpu.VMEM((6 * PLANE, SLOTS), BF16), pltpu.VMEM((6 * PLANE, SLOTS), BF16)],
        "force",
    )(returned.reshape(6 * PLANE, SLOTS), corner_slot, corner_weight, species, positions, velocities)
    moved, new_velocities = call(
        constrain_kernel,
        [((3, BEADS_DEV), F32), ((3, BEADS_DEV), F32)],
        [pltpu.VMEM((128, ENDS), BF16), pltpu.VMEM((128, ENDS), BF16)],
        "constrain",
    )(bond_pairs, bonds, delta, positions)
    return (moved, new_velocities, smoothed)


def solution(mesh):
    placed = (
        P(None, OWNERS),
        P(None, OWNERS),
        P(OWNERS),
        P(None, None, OWNERS),
        P(None, OWNERS),
        P(None, OWNERS, None),
        P(None, OWNERS),
    )
    return jax.shard_map(
        on_device,
        mesh=mesh,
        in_specs=placed,
        out_specs=(P(None, OWNERS), P(None, OWNERS), P(None, "bx", "by", "bz")),
        check_vma=False,
    )
```

time: 1120 us -> 175 us (0.16); the launches traced: 1110 us -> 175 us
  other arithmetic: 568 us -> 0 us
  local copies, waits for them, and re-layouts: 471 us -> 9.08 us
  Pallas kernels: 0 us -> 106 us
  blocking collectives: 6.69 us -> 23.7 us
  starting transfers between devices: 26.3 us -> 14.5 us
  waiting for transfers between devices: 32.9 us -> 21.5 us
    scatter-add x10 -> x0, other arithmetic: 500 us -> none  [the longest x8 221 us: constrain(): moved = moved.at[:, first].add(-shifted).at[:, second].add(shifted)]
    gather x13 -> x0, local copies, waits for them, and re-layouts: 377 us -> none  [the longest x1 112 us: on_device(): table[0][:, flat_slots].reshape(3, 8, count)]
    pallas_call x0 -> x9, Pallas kernels: none -> 106 us  [the longest x1 34.5 us: on_device(): call(lookup_kernel, ((6, PLANE, SLOTS), F32), [], 'lookup')]
    reshape x5 -> x0, local copies, waits for them, and re-layouts: 43.1 us -> none  [the longest x2 18.8 us: on_device(): slopes = jnp.stack([slope_x, slope_y, slope_z], axis=1).reshape(6, cells)]
    reduce_sum x5 -> x0, other arithmetic: 28.4 us -> none  [the longest x1 14.3 us: on_device(): force = -jnp.sum(corner_weight[None] * picked, axis=1)]
    mul x1 -> x0, other arithmetic: 22.3 us -> none  [on_device(): density = density * (CX * CY * CZ / BEADS_DEV)]
    all_to_all x1, blocking collectives: 6.69 us -> 23.7 us  [on_device(): lax.all_to_all(packets, PLANE_AXES, split_axis=0, concat_axis=0, tiled=True)]
    another operation x3 -> x0, local copies, waits for them, and re-layouts: 14.7 us -> none  [the longest x1 8.34 us: on_device(): jnp.stack([jnp.where(is_lipid, corner_weight, 0.0), jnp.where(is_lipid, 0...]
  transfers between devices with their start and end apart: 8 -> 7, of which waited for: 5 -> 5; matrix products, arithmetic and copies ran while one was open for 2% -> 0% of each run, Pallas kernels for 0% -> 3%
where the time goes in v1:
time: 175 us
  Pallas kernels  106 us (61%)
  blocking collectives  23.7 us (14%)
  waiting for transfers between devices  21.5 us (12%)
  starting transfers between devices  14.5 us (8%)
  local copies, waits for them, and re-layouts  9.08 us (5%)
    pallas_call x1, Pallas kernels, on_device(): call(lookup_kernel, ((6, PLANE, SLOTS), F32), [], 'lookup')  34.5 us
    all_to_all x1, blocking collectives, on_device(): lax.all_to_all(packets, PLANE_AXES, split_axis=0, concat_axis=0, tiled=True)  23.7 us
    pallas_call x1, Pallas kernels, on_device(): call(force_kernel, ((3, BEADS_DEV), F32), [pltpu.VMEM((6 * PLANE, SLOTS),...  17.5 us
    pallas_call x1, Pallas kernels, on_device(): call(pack_kernel, ((PLANE, 2 * SLOTS), F32), [pltpu.VMEM((256, SLOTS), F3...  13.2 us
    all_to_all x1, waiting for transfers between devices, on_device(): lax.all_to_all(outgoing, PLANE_AXES, split_axis=1, concat_axis=1, tiled=T...  12.7 us
    pallas_call x1, Pallas kernels, on_device(): call(spread_kernel, ((CX, CY, wide), F32), [pltpu.VMEM((CX * CY, SPREAD_R...  12.3 us
    pallas_call x1, Pallas kernels, on_device(): call(slopes_kernel, [((2, CX, CY, CZ), F32), ((6 * wide, CX * CY), BF16)]...  9.1 us
    ppermute x6, waiting for transfers between devices, neighbours(): return (lax.ppermute(tail, axis, up), lax.ppermute(head, axis, down))  8.73 us
  transfers between devices with their start and end apart: 7, of which 5 were waited for; matrix products, arithmetic and copies ran while one was open for 0% of the time, Pallas kernels for 3%

profile of v1, /device:TPU:1, one launch (start us, length us, event | category | flops | bytes accessed | tf_op | source)
XLA Modules:
  0.0 174.9 jit_solution(12584538296381941195)
XLA Ops:
  0.6 13.2 %pack.1 = f32[64,512]{1,0:T(8,128)} custom-call(s32[2,8,4096]{2,1,0:T(8,128)} %slot_ref.3, f32[8,4096]{1,0:T(8,128)} %weight_ref.3, s32[1,4096]{1,0:T(1,128)} %bitcast.9), custom_call_target="tpu_custom_call" | custom-call | tf_op jit(solution)/shard_map/pack/pallas_call | solution.py:415
  13.8 1.0 copy.12
  14.8 23.7 %all_to_all.16 = f32[64,1,512]{2,1,0:T(1,128)S(1)} all-to-all(f32[64,1,512]{2,1,0:T(1,128)S(1)} %copy.12), channel_id=1, replica_groups=mesh['bx'=8,'by'=8,'bz'=4] {'bx','by'}, dimensions={0} | all-to-all | bytes 262144 | tf_op jit(solution)/shard_map/all_to_all | solution.py:421
  38.5 0.7 copy.17
  39.2 12.3 %spread.1.own_ref = f32[16,64,128]{2,1,0:T(8,128)} custom-call(f32[64,512]{1,0:T(8,128)} %bitcast.7, s32[3,64,256]{2,1,0:T(8,128)} %cell_ref.3), custom_call_target="tpu_custom_call" | custom-call | tf_op jit(solution)/shard_map/spread/pallas_call | solution.py:422
  51.5 1.0 fusion
  52.5 0.5 collective-permute-start
  53.0 2.3 %collective-permute-start.1 = (f32[4,64,128]{2,1,0:T(8,128)S(1)}, f32[4,64,128]{2,1,0:T(8,128)S(1)}, u32[]{:S(2)}, u32[]{:S(2)}) collective-permute-start(f32[4,64,128]{2,1,0:T(8,128)S(1)} %get-tuple-element.21), channel_id=1, source_target_pairs={{32,0},{64,32},{96,64},{128,96},{160,128},{192,160},{224,192},{0,2... | collective-permute-start | bytes 393224 | tf_op jit(solution)/shard_map/ppermute | solution.py:408
  55.2 3.2 %collective-permute-done.left_ref = f32[4,64,128]{2,1,0:T(8,128)S(1)} collective-permute-done((f32[4,64,128]{2,1,0:T(8,128)S(1)}, f32[4,64,128]{2,1,0:T(8,128)S(1)}, u32[]{:S(2)}, u32[]{:S(2)}) %collective-permute-start) | collective-permute-done | bytes 131104 | tf_op jit(solution)/shard_map/ppermute | solution.py:408
  58.4 0.0 copy-start
  58.4 0.0 collective-permute-done.1.right_ref
  58.4 0.6 copy-done
  59.1 0.0 copy-start.1
  59.1 0.7 copy-done.1
  59.7 2.4 %filter_x.1 = (f32[18,64,128]{2,1,0:T(8,128)}, f32[18,4,128]{2,1,0:T(4,128)}, f32[18,4,128]{2,1,0:T(4,128)}) custom-call(f32[4,64,128]{2,1,0:T(8,128)} %copy-done, f32[16,64,128]{2,1,0:T(8,128)} %spread.1.own_ref, f32[4,64,128]{2,1,0:T(8,128)} %copy-done.1), custom_call_target="tpu_custom_call" | custom-call | tf_op jit(solution)/shard_map/filter_x/pallas_call | solution.py:433
  62.2 1.3 collective-permute-start.2
  63.5 0.0 collective-permute-start.3
  63.5 1.4 collective-permute-done.2.left_ref
  64.9 0.0 copy-start.4
  64.9 2.5 %collective-permute-done.3.right_ref = f32[18,4,128]{2,1,0:T(4,128)S(1)} collective-permute-done((f32[18,4,128]{2,1,0:T(4,128)}, f32[18,4,128]{2,1,0:T(4,128)S(1)}, u32[]{:S(2)}, u32[]{:S(2)}) %collective-permute-start.3) | collective-permute-done | bytes 36896 | tf_op jit(solution)/shard_map/ppermute | solution.py:408
  67.4 0.0 copy-start.5
  67.4 0.0 copy-done.4
  67.4 0.6 copy-done.5
  68.0 4.9 %filter_y.1 = (f32[18,72,128]{2,1,0:T(8,128)}, f32[18,16,72]{2,1,0:T(8,128)}) custom-call(f32[18,4,128]{2,1,0:T(4,128)} %copy-done.4, f32[18,64,128]{2,1,0:T(8,128)} %get-tuple-element.13.own_ref, f32[18,4,128]{2,1,0:T(4,128)} %copy-done.5), custom_call_target="tpu_custom_call" | custom-call | tf_op jit(solution)/shard_map/filter_y/pallas_call | solution.py:440
  72.9 0.9 fusion.1
  73.8 1.3 collective-permute-start.4
  75.1 1.7 collective-permute-start.5
  76.8 1.7 collective-permute-done.4.left_ref
  78.5 0.0 copy-start.2
  78.5 0.0 collective-permute-done.5.right_ref
  78.5 0.0 copy-start.3
  78.5 0.6 copy-done.2
  79.1 0.0 copy-done.3
  79.1 9.1 %slopes.1 = (f32[2,16,64,64]{3,2,1,0:T(8,128)}, bf16[768,1024]{1,0:T(8,128)(2,1)}) custom-call(f32[18,72,128]{2,1,0:T(8,128)} %get-tuple-element.15.own_ref, f32[18,8,72]{2,1,0:T(8,128)} %copy-done.2, f32[18,8,72]{2,1,0:T(8,128)} %copy-done.3, f32[128,384]{1,0:T(8,128)} %constant.4.clone.op_ref, f32[16,384]{1,0:T(8,128)} %constant.5.clone.hop_ref), custom_call_target="tpu_custom_call" | custom-call | tf_op jit(solution)/shard_map/slopes/pallas_call | solution.py:448
  88.2 34.5 %lookup.1 = f32[6,64,256]{2,1,0:T(8,128)} custom-call(bf16[768,1024]{1,0:T(8,128)(2,1)} %get-tuple-element.17.table_ref, s32[3,64,256]{2,1,0:T(8,128)} %cell_ref.3), custom_call_target="tpu_custom_call" | custom-call | tf_op jit(solution)/shard_map/lookup/pallas_call | solution.py:454
  122.7 2.0 %copy.13 = f32[6,64,256]{2,0,1:T(8,128)} copy(f32[6,64,256]{2,1,0:T(8,128)} %lookup.1) | data formatting | bytes 786432 | tf_op jit(solution)/shard_map/lookup/pallas_call | solution.py:454
  124.8 7.4 %all-to-all-start.1 = ((f32[6,64,256]{2,0,1:T(8,128)}), f32[6,64,256]{2,0,1:T(8,128)S(1)}, u32[]{:S(2)}, u32[]{:S(2)}) async-start(f32[6,64,256]{2,0,1:T(8,128)} %copy.13), calls=%async_computation.1 | async-start | bytes 1048576 | tf_op jit(solution)/shard_map/all_to_all | solution.py:455
  132.2 4.9 %bonds.1.bonds_ref = f32[8,3840]{1,0:T(8,128)} custom-call(s32[2,3840]{1,0:T(2,128)} %pairs_ref.3, f32[3,4096]{1,0:T(4,128)} %pos_ref.3), custom_call_target="tpu_custom_call" | custom-call | tf_op jit(solution)/shard_map/bonds/pallas_call | solution.py:418
  137.1 12.7 %all-to-all-done.1 = f32[6,64,256]{2,0,1:T(8,128)S(1)} async-done(((f32[6,64,256]{2,0,1:T(8,128)}), f32[6,64,256]{2,0,1:T(8,128)S(1)}, u32[]{:S(2)}, u32[]{:S(2)}) %all-to-all-start.1) | async-done | bytes 393248 | tf_op jit(solution)/shard_map/all_to_all | solution.py:455
  149.9 0.9 copy.14
  150.7 17.5 %force.1.delta_ref = f32[3,4096]{1,0:T(4,128)} custom-call(f32[384,256]{1,0:T(8,128)} %bitcast.6, s32[2,8,4096]{2,1,0:T(8,128)} %slot_ref.3, f32[8,4096]{1,0:T(8,128)} %weight_ref.3, s32[1,4096]{1,0:T(1,128)} %bitcast.10, f32[3,4096]{1,0:T(4,128)} %pos_ref.3, f32[3,4096]{1,0:T(4,128)} %vel_ref.1), custom_call_target="tpu_custom_call" | custom-call | tf_op jit(solution)/shard_map/force/pallas_call | solution.py:456
  168.3 6.7 %constrain.1 = (f32[3,4096]{1,0:T(4,128)}, f32[3,4096]{1,0:T(4,128)}) custom-call(s32[2,3840]{1,0:T(2,128)} %pairs_ref.3, f32[8,3840]{1,0:T(8,128)} %bonds.1.bonds_ref, f32[3,4096]{1,0:T(4,128)} %force.1.delta_ref, f32[3,4096]{1,0:T(4,128)} %pos_ref.3), custom_call_target="tpu_custom_call" | custom-call | tf_op jit(solution)/shard_map/constrain/pallas_call | solution.py:462
Async XLA Ops:
  52.5 5.9 %collective-permute-start = (f32[4,64,128]{2,1,0:T(8,128)S(1)}, f32[4,64,128]{2,1,0:T(8,128)S(1)}, u32[]{:S(2)}, u32[]{:S(2)}) collective-permute-start(f32[4,64,128]{2,1,0:T(8,128)S(1)} %get-tuple-element.22), channel_id=1, source_target_pairs={{0,32},{32,64},{64,96},{96,128},{128,160},{160,192},{192,224},{224... | collective-permute-start | bytes 393224 | tf_op jit(solution)/shard_map/ppermute | solution.py:408
  53.0 5.5 %collective-permute-start.1 = (f32[4,64,128]{2,1,0:T(8,128)S(1)}, f32[4,64,128]{2,1,0:T(8,128)S(1)}, u32[]{:S(2)}, u32[]{:S(2)}) collective-permute-start(f32[4,64,128]{2,1,0:T(8,128)S(1)} %get-tuple-element.21), channel_id=1, source_target_pairs={{32,0},{64,32},{96,64},{128,96},{160,128},{192,160},{224,192},{0,2... | collective-permute-start | bytes 393224 | tf_op jit(solution)/shard_map/ppermute | solution.py:408
  58.4 0.6 copy-start
  59.1 0.7 copy-start.1
  62.2 2.7 %collective-permute-start.2 = (f32[18,4,128]{2,1,0:T(4,128)}, f32[18,4,128]{2,1,0:T(4,128)S(1)}, u32[]{:S(2)}, u32[]{:S(2)}) collective-permute-start(f32[18,4,128]{2,1,0:T(4,128)} %get-tuple-element.12), channel_id=1, source_target_pairs={{0,4},{4,8},{8,12},{12,16},{16,20},{20,24},{24,28},{28,0},{1,5},{5... | collective-permute-start | bytes 110600 | tf_op jit(solution)/shard_map/ppermute | solution.py:408
  63.5 3.9 %collective-permute-start.3 = (f32[18,4,128]{2,1,0:T(4,128)}, f32[18,4,128]{2,1,0:T(4,128)S(1)}, u32[]{:S(2)}, u32[]{:S(2)}) collective-permute-start(f32[18,4,128]{2,1,0:T(4,128)} %get-tuple-element.14), channel_id=1, source_target_pairs={{4,0},{8,4},{12,8},{16,12},{20,16},{24,20},{28,24},{0,28},{5,1},{9... | collective-permute-start | bytes 110600 | tf_op jit(solution)/shard_map/ppermute | solution.py:408
  64.9 2.5 %copy-start.4 = (f32[18,4,128]{2,1,0:T(4,128)}, f32[18,4,128]{2,1,0:T(4,128)S(1)}, u32[]{:S(2)}) copy-start(f32[18,4,128]{2,1,0:T(4,128)S(1)} %collective-permute-done.2.left_ref) | copy-start | bytes 110596
  67.4 0.6 copy-start.5
  73.8 4.7 %collective-permute-start.4 = (f32[18,8,72]{2,1,0:T(8,128)S(1)}, f32[18,8,72]{2,1,0:T(8,128)S(1)}, u32[]{:S(2)}, u32[]{:S(2)}) collective-permute-start(f32[18,8,72]{2,1,0:T(8,128)S(1)} %get-tuple-element.24), channel_id=1, source_target_pairs={{0,1},{1,2},{2,3},{3,0},{4,5},{5,6},{6,7},{7,4},{8,9},{9,10},{10,1... | collective-permute-start | bytes 124424 | tf_op jit(solution)/shard_map/ppermute | solution.py:408
  75.1 3.4 %collective-permute-start.5 = (f32[18,8,72]{2,1,0:T(8,128)S(1)}, f32[18,8,72]{2,1,0:T(8,128)S(1)}, u32[]{:S(2)}, u32[]{:S(2)}) collective-permute-start(f32[18,8,72]{2,1,0:T(8,128)S(1)} %get-tuple-element.23), channel_id=1, source_target_pairs={{1,0},{2,1},{3,2},{0,3},{5,4},{6,5},{7,6},{4,7},{9,8},{10,9},{11,1... | collective-permute-start | bytes 124424 | tf_op jit(solution)/shard_map/ppermute | solution.py:408
  78.5 0.6 copy-start.2
  78.5 0.6 copy-start.3
  124.8 25.1 %all-to-all-start.1 = ((f32[6,64,256]{2,0,1:T(8,128)}), f32[6,64,256]{2,0,1:T(8,128)S(1)}, u32[]{:S(2)}, u32[]{:S(2)}) async-start(f32[6,64,256]{2,0,1:T(8,128)} %copy.13), calls=%async_computation.1 | async-start | bytes 1048576 | tf_op jit(solution)/shard_map/all_to_all | solution.py:455

commit v2 on v1

v2 whole, which is shorter than its diff:
```python
import functools
import math

import jax
import jax.numpy as jnp
import numpy as np
from jax import lax
from jax.experimental import pallas as pl
from jax.experimental.pallas import tpu as pltpu
from jax.sharding import PartitionSpec as P

CX = 16
CY = 64
CZ = 64
BEADS_DEV = 4096
REACH = 3
SWEEPS = 4
SLOTS = 256
PLANE = 64
BONDS_DEV = 3840
OWNERS = ("bx", "by", "bz")
N_BY = 8
MESH = pl.DeviceIdType.MESH
PACK_CHUNK = 1024
SPREAD_ROWS = 8
GATHER_ROWS = 2
FORCE_CHUNK = 512
YP = 72
W = REACH + 1
WIDE = 2 * CZ
HALF = BONDS_DEV
ENDS = 2 * BONDS_DEV

spread_cells = 1.0
mixing = 10.0
stiffness = 5.0
time_step = 0.1

F32 = jnp.float32
BF16 = jnp.bfloat16
NT = (((1,), (1,)), ((), ()))
NN = (((1,), (0,)), ((), ()))


def gauss_taps():
    raw_list = [
        math.exp(-0.5 * (offset - REACH) ** 2 / spread_cells**2) for offset in range(2 * REACH + 1)
    ]
    tap_total = sum(raw_list)
    return [entry / tap_total for entry in raw_list]


def mm(a, b, dims=NN):
    return lax.dot_general(a, b, dims, preferred_element_type=F32)


def two(x):
    hi = x.astype(BF16)
    return hi, (x - hi.astype(F32)).astype(BF16)


def three(x):
    hi = x.astype(BF16)
    rest = x - hi.astype(F32)
    mid = rest.astype(BF16)
    return hi, mid, (rest - mid.astype(F32)).astype(BF16)


def rows_iota(rows, n, dtype=BF16):
    return lax.broadcasted_iota(jnp.int32, (rows, n), 0).astype(F32).astype(dtype)


def onehot(index, rows):
    return jnp.where(
        rows_iota(rows, index.shape[1]) == index.astype(F32).astype(BF16),
        jnp.ones((), BF16),
        jnp.zeros((), BF16),
    )


def weighted(index, rows, value):
    return jnp.where(
        rows_iota(rows, index.shape[1]) == index.astype(F32).astype(BF16),
        value,
        jnp.zeros((), BF16),
    )


def pick(index, rows, values):
    n = index.shape[1]
    mask = lax.broadcasted_iota(jnp.int32, (rows, n), 0) == index
    return [
        jnp.sum(jnp.where(mask, values[g * rows : (g + 1) * rows], 0.0), axis=0, keepdims=True)
        for g in range(values.shape[0] // rows)
    ]


def onehot_xy(x, y):
    oy = onehot(y, CY)
    xb = x.astype(F32).astype(BF16)
    zero = jnp.zeros((), BF16)
    blocks = []
    for i in range(CX):
        blocks.append(jnp.where(xb == jnp.asarray(i, BF16), oy, zero))
    return jnp.concatenate(blocks, axis=0)


def z_operators():
    taps = gauss_taps()
    w = REACH + 1
    smooth = np.zeros((CZ + 2 * w, CZ))
    slope = np.zeros((CZ + 2 * w, CZ))
    for z in range(CZ):
        for j in range(2 * REACH + 1):
            smooth[z + w + j - REACH, z] += taps[j]
            slope[z + w + 1 + j - REACH, z] += 0.5 * taps[j]
            slope[z + w - 1 + j - REACH, z] -= 0.5 * taps[j]
    mix = np.array([[stiffness, mixing + stiffness], [mixing + stiffness, stiffness]])
    full = np.concatenate(
        [np.kron(np.eye(2), smooth), np.kron(mix.T, smooth), np.kron(mix.T, slope)], axis=1
    ).reshape(2, CZ + 2 * w, 6 * CZ)
    own = full[:, w : w + CZ].reshape(2 * CZ, 6 * CZ)
    halo = np.concatenate(
        [full[:, :w].reshape(2 * w, 6 * CZ), full[:, w + CZ :].reshape(2 * w, 6 * CZ)]
    )
    return own.astype(np.float32), halo.astype(np.float32)


def mm3(a, b_hi, b_lo):
    a_hi, a_lo = two(a)
    return mm(a_hi, b_hi) + (mm(a_hi, b_lo) + mm(a_lo, b_hi))


def to_rows(x):
    return jnp.concatenate([x[:, i : i + 128] for i in range(0, x.shape[1], 128)], axis=0)


def to_line(x):
    return jnp.concatenate([x[i : i + 1] for i in range(x.shape[0])], axis=1)


def pack(slot_ref, weight_ref, species_ref, send_ref, acc_ref):
    acc_ref[...] = jnp.zeros_like(acc_ref)

    def body(step, carry):
        c = step % 8
        cols = pl.ds(pl.multiple_of((step // 8) * PACK_CHUNK, PACK_CHUNK), PACK_CHUNK)
        brick = slot_ref[0, pl.ds(c, 1), cols]
        slot = slot_ref[1, pl.ds(c, 1), cols]
        kd = brick + PLANE * species_ref[:, cols]
        hi, lo = two(weight_ref[pl.ds(c, 1), cols])
        left = jnp.concatenate([weighted(kd, 2 * PLANE, hi), weighted(kd, 2 * PLANE, lo)], axis=0)
        acc_ref[...] += mm(left, onehot(slot, SLOTS), NT)
        return carry

    lax.fori_loop(0, 8 * BEADS_DEV // PACK_CHUNK, body, 0)
    total = acc_ref[: 2 * PLANE] + acc_ref[2 * PLANE :]
    send_ref[:, 0, :] = total[:PLANE]
    send_ref[:, 1, :] = total[PLANE:]


def spread(me, arrive, recv_ref, cell_ref, ext_ref, xy_ref, z_ref, acc_ref):
    acc_ref[...] = jnp.zeros_like(acc_ref)

    def body(step, carry):
        for i in range(SPREAD_ROWS):
            t = step * SPREAD_ROWS + i
            p = lax.rem(me - t + PLANE, PLANE)
            arrive(t, p)
            x, y, z = (cell_ref[a, pl.ds(p, 1), :] for a in range(3))
            cols = slice(i * SLOTS, (i + 1) * SLOTS)
            xy_ref[:, cols] = onehot_xy(x, y)
            for k in range(2):
                hi, lo = two(recv_ref[p, k : k + 1, :])
                z_ref[k * CZ : (k + 1) * CZ, cols] = weighted(z, CZ, hi)
                z_ref[(2 + k) * CZ : (3 + k) * CZ, cols] = weighted(z, CZ, lo)
        acc_ref[...] += mm(xy_ref[...], z_ref[...], NT)
        return carry

    lax.fori_loop(0, PLANE // SPREAD_ROWS, body, 0)
    total = (acc_ref[:, :WIDE] + acc_ref[:, WIDE:]) * (CX * CY * CZ / BEADS_DEV)
    ext_ref[W : W + CX] = total.reshape(CX, CY, WIDE)


def filter_x(ext_ref, ey_ref, head_ref, tail_ref):
    taps = gauss_taps()

    def body(i, carry):
        total = taps[0] * ext_ref[i]
        for j in range(1, 2 * REACH + 1):
            total = total + taps[j] * ext_ref[i + j]
        ey_ref[i, W : W + CY] = total
        head_ref[i] = total[:W]
        tail_ref[i] = total[CY - W :]
        return carry

    lax.fori_loop(0, CX + 2, body, 0)


def filter_y(left_ref, right_ref, ey_ref, ay_ref, head_ref, tail_ref):
    taps = gauss_taps()
    span = CY + 2
    row = lax.broadcasted_iota(jnp.int32, (16, WIDE), 0)
    lane = lax.broadcasted_iota(jnp.int32, (16, WIDE), 1)
    wanted = ((row % 8) // W) * CZ + (row // 8) * (CZ - W) + row % W
    select = jnp.where(lane == wanted, 1.0, 0.0).astype(BF16)
    ey_ref[:, :W] = left_ref[...]
    ey_ref[:, W + CY :] = right_ref[...]

    def body(i, carry):
        total = taps[0] * ey_ref[i, :span]
        for j in range(1, 2 * REACH + 1):
            total = total + taps[j] * ey_ref[i, j : j + span]
        full = jnp.concatenate([total, jnp.zeros((YP - span, WIDE), F32)], axis=0)
        ay_ref[i] = full
        hi, mid, lo = three(full)
        edge = mm(select, hi, NT) + mm(select, mid, NT) + mm(select, lo, NT)
        head_ref[i] = edge[:8]
        tail_ref[i] = edge[8:]
        return carry

    lax.fori_loop(0, CX + 2, body, 0)


def slopes(left_ref, right_ref, op_ref, hop_ref, ay_ref, smooth_ref, table_ref, p_ref, pz_ref):
    op_hi, op_lo = two(op_ref[...])
    hop_hi, hop_lo = two(hop_ref[...])

    def filter_z(i, carry):
        halo = jnp.concatenate([left_ref[i], right_ref[i]], axis=0).T
        both = mm3(ay_ref[i], op_hi, op_lo) + mm3(halo, hop_hi, hop_lo)
        p_ref[i] = both[:, WIDE : 2 * WIDE]
        pz_ref[i] = both[:, 2 * WIDE :]

        @pl.when((i > 0) & (i <= CX))
        def _():
            for k in range(2):
                smooth_ref[k, i - 1] = both[1 : CY + 1, k * CZ : (k + 1) * CZ]

        return carry

    lax.fori_loop(0, CX + 2, filter_z, 0)

    for i in range(0, CX, 2):
        parts = []
        for q in (i + 1, i + 2):
            sx = (p_ref[q + 1, 1 : CY + 1] - p_ref[q - 1, 1 : CY + 1]) * 0.5
            sy = (p_ref[q, 2 : CY + 2] - p_ref[q, :CY]) * 0.5
            sz = pz_ref[q, 1 : CY + 1]
            parts.append((sx, sy, sz))
        cols = slice(i * CY, (i + 2) * CY)
        for a in range(3):
            hi, lo = two(jnp.concatenate([parts[0][a], parts[1][a]], axis=0).T)
            table_ref[a * WIDE : (a + 1) * WIDE, cols] = hi
            table_ref[(3 + a) * WIDE : (4 + a) * WIDE, cols] = lo


def lookup(me, leave, table_ref, cell_ref, send_ref):
    def body(step, carry):
        owners = [lax.rem(me + 1 + step * GATHER_ROWS + i, PLANE) for i in range(GATHER_ROWS)]
        xyz = [
            jnp.concatenate([cell_ref[a, pl.ds(p, 1), :] for p in owners], axis=1)
            for a in range(3)
        ]
        both = mm(table_ref[...], onehot_xy(xyz[0], xyz[1]))
        half = 6 * CZ
        found = pick(xyz[2], CZ, both[:half] + both[half:])
        for i, p in enumerate(owners):
            cols = slice(i * SLOTS, (i + 1) * SLOTS)
            send_ref[p] = jnp.concatenate([found[g][:, cols] for g in range(6)], axis=0)
        for p in owners:
            leave(p)
        return carry

    lax.fori_loop(0, PLANE // GATHER_ROWS, body, 0)


def forces(
    recv_ref, slot_ref, weight_ref, species_ref, vel_ref, delta_ref, hi_ref, lo_ref
):
    for g in range(6):
        hi, lo = two(recv_ref[:, g, :])
        hi_ref[g * PLANE : (g + 1) * PLANE] = hi
        lo_ref[g * PLANE : (g + 1) * PLANE] = lo
    wide = 2 * PLANE

    def body(step, carry):
        cols = pl.ds(pl.multiple_of(step * FORCE_CHUNK, FORCE_CHUNK), FORCE_CHUNK)
        species = species_ref[:, cols]
        force = [jnp.zeros((1, FORCE_CHUNK), F32)] * 3
        for c in range(8):
            oh = onehot(slot_ref[1, c : c + 1, cols], SLOTS)
            both = mm(hi_ref[...], oh) + mm(lo_ref[...], oh)
            found = pick(slot_ref[0, c : c + 1, cols] + PLANE * species, wide, both)
            weight = weight_ref[c : c + 1, cols]
            force = [force[a] - weight * found[a] for a in range(3)]
        for a in range(3):
            half = vel_ref[a : a + 1, cols] + 0.5 * time_step * force[a]
            delta_ref[a : a + 1, cols] = time_step * half
        return carry

    lax.fori_loop(0, BEADS_DEV // FORCE_CHUNK, body, 0)


def bonds(pairs_ref, positions_ref, out_ref, oh_ref):
    pairs = jnp.concatenate([pairs_ref[0:1], pairs_ref[1:2]], axis=1)
    hi_index = pairs >> 7
    oh_ref[...] = onehot(pairs & 127, 128)
    number = lax.broadcasted_iota(jnp.int32, (1, HALF), 1)
    number = jnp.concatenate([number, number], axis=1)
    sign = jnp.where(lax.broadcasted_iota(jnp.int32, (1, ENDS), 1) < HALF, 1.0, -1.0)
    left = jnp.concatenate(
        [
            weighted(hi_index, 32, v.astype(F32).astype(BF16))
            for v in (number >> 6, number & 63, sign)
        ],
        axis=0,
    )
    sums = mm(left, oh_ref[...], NT).astype(BF16)
    high, low, signs = pick(hi_index, 32, mm(sums, oh_ref[...]))
    other = 64.0 * high + low - number.astype(F32)
    other_sign = signs - sign
    parts = [three(to_rows(positions_ref[a : a + 1])) for a in range(3)]
    table = [jnp.concatenate([parts[a][q] for a in range(3)], axis=0) for q in range(3)]
    oh = oh_ref[...]
    ends = pick(hi_index, 32, mm(table[0], oh) + mm(table[1], oh) + mm(table[2], oh))
    for a in range(3):
        out_ref[a : a + 1] = ends[a][:, :HALF] - ends[a][:, HALF:]
    out_ref[3:4] = other[:, :HALF]
    out_ref[4:5] = other[:, HALF:]
    out_ref[5:6] = other_sign[:, :HALF]
    out_ref[6:7] = other_sign[:, HALF:]
    out_ref[7:8] = jnp.zeros((1, HALF), F32)


def constrain(pairs_ref, bonds_ref, delta_ref, pos_ref, newpos_ref, newvel_ref, oh_ref, nb_ref):
    pairs = jnp.concatenate([pairs_ref[0:1], pairs_ref[1:2]], axis=1)
    hi_index = pairs >> 7
    r = [bonds_ref[a : a + 1] for a in range(3)]
    other = jnp.concatenate([bonds_ref[3:4], bonds_ref[4:5]], axis=1).astype(jnp.int32)
    sign = [bonds_ref[5:6], bonds_ref[6:7]]
    other_hi = other >> 7
    nb_ref[...] = onehot(other & 127, 128)
    delta = [delta_ref[a : a + 1] for a in range(3)]
    parts = [two(to_rows(d)) for d in delta]
    table = [jnp.concatenate([parts[a][q] for a in range(3)], axis=0) for q in range(2)]
    ends = pick(hi_index, 32, mm(table[0], oh_ref[...]) + mm(table[1], oh_ref[...]))
    v = [r[a] + (ends[a][:, :HALF] - ends[a][:, HALF:]) for a in range(3)]
    total = [jnp.zeros((1, HALF), F32)] * 3
    for sweep in range(SWEEPS):
        vv = v[0] * v[0] + v[1] * v[1] + v[2] * v[2]
        vr = v[0] * r[0] + v[1] * r[1] + v[2] * r[2]
        g = (vv - 1.0) / (4.0 * jnp.maximum(vr, 0.5))
        shift = [g * r[a] for a in range(3)]
        total = [total[a] + shift[a] for a in range(3)]
        if sweep + 1 == SWEEPS:
            break
        pad = jnp.zeros((2, 128), F32)
        parts = [two(jnp.concatenate([to_rows(s), pad], axis=0)) for s in shift]
        table = [jnp.concatenate([parts[a][q] for a in range(3)], axis=0) for q in range(2)]
        near = pick(other_hi, 32, mm(table[0], nb_ref[...]) + mm(table[1], nb_ref[...]))
        v = [
            v[a] - 2.0 * shift[a] - sign[0] * near[a][:, :HALF] + sign[1] * near[a][:, HALF:]
            for a in range(3)
        ]
    rows = []
    for a in range(3):
        both = jnp.concatenate([total[a], -total[a]], axis=1)
        rows += [weighted(hi_index, 32, q) for q in two(both)]
    moved = mm(jnp.concatenate(rows, axis=0), oh_ref[...], NT)
    for a in range(3):
        q = to_line(moved[64 * a : 64 * a + 32] + moved[64 * a + 32 : 64 * a + 64])
        change = delta[a] - q
        newpos_ref[a : a + 1] = pos_ref[a : a + 1] + change
        newvel_ref[a : a + 1] = change / time_step


def step_kernel(
    slot_ref,
    weight_ref,
    species_ref,
    cell_ref,
    pairs_ref,
    pos_ref,
    vel_ref,
    op_ref,
    hop_ref,
    newpos_ref,
    newvel_ref,
    smooth_ref,
    acc1_ref,
    send1_ref,
    recv1_ref,
    xy_ref,
    z_ref,
    acc2_ref,
    ext_ref,
    ey_ref,
    yside_ref,
    ay_ref,
    zside_ref,
    p_ref,
    pz_ref,
    table_ref,
    send2_ref,
    recv2_ref,
    hi_ref,
    lo_ref,
    delta_ref,
    bonds_ref,
    oh_ref,
    nb_ref,
    out_sem,
    in_sem,
    back_out_sem,
    back_in_sem,
    side_out_sem,
    side_in_sem,
):
    bx, by, bz = (lax.axis_index(a) for a in OWNERS)
    me = bx * N_BY + by
    counts = [lax.axis_size(a) for a in OWNERS]

    def owner(p):
        return (p // N_BY, lax.rem(p, N_BY), bz)

    def shifted(axis, by_how):
        place = [bx, by, bz]
        place[axis] = lax.rem(place[axis] + by_how + counts[axis], counts[axis])
        return tuple(place)

    barrier = pltpu.get_barrier_semaphore()

    def greet(t, carry):
        p = lax.rem(me + t, PLANE)
        pl.semaphore_signal(barrier, inc=1, device_id=owner(p), device_id_type=MESH)
        return carry

    lax.fori_loop(1, PLANE, greet, 0)
    for by_how in (-1, 1):
        pl.semaphore_signal(barrier, inc=1, device_id=shifted(2, by_how), device_id_type=MESH)

    pack(slot_ref, weight_ref, species_ref, send1_ref, acc1_ref)
    pl.semaphore_wait(barrier, PLANE + 1)

    def packet(send_ref, recv_ref, out, into, p, source):
        return pltpu.make_async_remote_copy(
            src_ref=send_ref.at[p],
            dst_ref=recv_ref.at[source],
            send_sem=out.at[p],
            recv_sem=into.at[source],
            device_id=owner(p),
            device_id_type=MESH,
        )

    def forward(p, source):
        return packet(send1_ref, recv1_ref, out_sem, in_sem, p, source)

    def back(p, source):
        return packet(send2_ref, recv2_ref, back_out_sem, back_in_sem, p, source)

    def send(t, carry):
        forward(lax.rem(me + t, PLANE), me).start()
        return carry

    lax.fori_loop(1, PLANE, send, 0)
    recv1_ref[me] = send1_ref[me]
    bonds(pairs_ref, pos_ref, bonds_ref, oh_ref)

    def arrive(t, p):
        @pl.when(t > 0)
        def _():
            forward(p, p).wait_recv()

    spread(me, arrive, recv1_ref, cell_ref, ext_ref, xy_ref, z_ref, acc2_ref)

    def exchange(axis, to_left, to_right, from_left, from_right):
        copies = [
            pltpu.make_async_remote_copy(
                src_ref=src,
                dst_ref=dst,
                send_sem=side_out_sem.at[2 * axis + n],
                recv_sem=side_in_sem.at[2 * axis + n],
                device_id=shifted(axis, by_how),
                device_id_type=MESH,
            )
            for n, (src, dst, by_how) in enumerate(
                ((to_left, from_right, -1), (to_right, from_left, 1))
            )
        ]
        for copy in copies:
            copy.start()
        for copy in copies:
            copy.wait()

    exchange(
        0,
        ext_ref.at[pl.ds(W, W)],
        ext_ref.at[pl.ds(CX, W)],
        ext_ref.at[pl.ds(0, W)],
        ext_ref.at[pl.ds(W + CX, W)],
    )
    filter_x(ext_ref, ey_ref, yside_ref.at[0], yside_ref.at[1])
    exchange(1, *(yside_ref.at[n] for n in range(4)))
    filter_y(yside_ref.at[2], yside_ref.at[3], ey_ref, ay_ref, zside_ref.at[0], zside_ref.at[1])
    exchange(2, *(zside_ref.at[n] for n in range(4)))
    slopes(
        zside_ref.at[2],
        zside_ref.at[3],
        op_ref,
        hop_ref,
        ay_ref,
        smooth_ref,
        table_ref,
        p_ref,
        pz_ref,
    )

    def leave(p):
        @pl.when(p != me)
        def _():
            back(p, me).start()

    lookup(me, leave, table_ref, cell_ref, send2_ref)
    recv2_ref[me] = send2_ref[me]

    def finish(t, carry):
        p = lax.rem(me + t, PLANE)
        forward(p, me).wait_send()
        back(p, me).wait_send()
        source = lax.rem(me - t + PLANE, PLANE)
        back(source, source).wait_recv()
        return carry

    lax.fori_loop(1, PLANE, finish, 0)
    forces(
        recv2_ref, slot_ref, weight_ref, species_ref, vel_ref, delta_ref, hi_ref, lo_ref
    )
    constrain(pairs_ref, bonds_ref, delta_ref, pos_ref, newpos_ref, newvel_ref, oh_ref, nb_ref)


def on_device(positions, velocities, species, corner_slot, corner_weight, slot_cell, bond_pairs):
    own_op, halo_op = z_operators()
    layers = CX + 2
    scratch = [
        ((256, SLOTS), F32),
        ((PLANE, 2, SLOTS), F32),
        ((PLANE, 2, SLOTS), F32),
        ((CX * CY, SPREAD_ROWS * SLOTS), BF16),
        ((4 * CZ, SPREAD_ROWS * SLOTS), BF16),
        ((CX * CY, 4 * CZ), F32),
        ((CX + 2 * W, CY, WIDE), F32),
        ((layers, CY + 2 * W, WIDE), F32),
        ((4, layers, W, WIDE), F32),
        ((layers, YP, WIDE), F32),
        ((4, layers, 8, YP), F32),
        ((layers, YP, WIDE), F32),
        ((layers, YP, WIDE), F32),
        ((6 * WIDE, CX * CY), BF16),
        ((PLANE, 6, SLOTS), F32),
        ((PLANE, 6, SLOTS), F32),
        ((6 * PLANE, SLOTS), BF16),
        ((6 * PLANE, SLOTS), BF16),
        ((3, BEADS_DEV), F32),
        ((8, BONDS_DEV), F32),
        ((128, ENDS), BF16),
        ((128, ENDS), BF16),
    ]
    vmem = pl.BlockSpec(memory_space=pltpu.VMEM)
    outs = [((3, BEADS_DEV), F32), ((3, BEADS_DEV), F32), ((2, CX, CY, CZ), F32)]
    dma = pltpu.SemaphoreType.DMA
    moved, new_velocities, smoothed = pl.pallas_call(
        step_kernel,
        out_shape=[jax.ShapeDtypeStruct(*o) for o in outs],
        in_specs=[vmem] * 9,
        out_specs=[vmem] * 3,
        scratch_shapes=[pltpu.VMEM(*s) for s in scratch] + [dma((PLANE,))] * 4 + [dma((6,))] * 2,
        compiler_params=pltpu.CompilerParams(
            vmem_limit_bytes=60 * 1024 * 1024, collective_id=0, has_side_effects=True
        ),
        name="step",
    )(
        corner_slot,
        corner_weight,
        species[None, :],
        slot_cell,
        bond_pairs,
        positions,
        velocities,
        jnp.asarray(own_op),
        jnp.asarray(halo_op),
    )
    return (moved, new_velocities, smoothed)


def solution(mesh):
    placed = (
        P(None, OWNERS),
        P(None, OWNERS),
        P(OWNERS),
        P(None, None, OWNERS),
        P(None, OWNERS),
        P(None, OWNERS, None),
        P(None, OWNERS),
    )
    return jax.shard_map(
        on_device,
        mesh=mesh,
        in_specs=placed,
        out_specs=(P(None, OWNERS), P(None, OWNERS), P(None, "bx", "by", "bz")),
        check_vma=False,
    )
```

time: 175 us -> 130 us (0.74)
  blocking collectives: 23.7 us -> 0 us
  waiting for transfers between devices: 21.5 us -> 0 us
  Pallas kernels: 106 us -> 125 us
  starting transfers between devices: 14.5 us -> 0 us
  local copies, waits for them, and re-layouts: 9.08 us -> 4.45 us
    all_to_all x1 -> x0, blocking collectives: 23.7 us -> none  [on_device(): lax.all_to_all(packets, PLANE_AXES, split_axis=0, concat_axis=0, tiled=True)]
    pallas_call x9 -> x1, Pallas kernels: 106 us -> 125 us  [on_device(): pl.pallas_call(step_kernel, out_shape=[jax.ShapeDtypeStruct(*o) for o in...]
    all_to_all x1 -> x0, waiting for transfers between devices: 12.7 us -> none  [on_device(): lax.all_to_all(outgoing, PLANE_AXES, split_axis=1, concat_axis=1, tiled=T...]
    ppermute x6 -> x0, waiting for transfers between devices: 8.73 us -> none  [neighbours(): return (lax.ppermute(tail, axis, up), lax.ppermute(head, axis, down))]
    all_to_all x1 -> x0, starting transfers between devices: 7.39 us -> none  [on_device(): lax.all_to_all(outgoing, PLANE_AXES, split_axis=1, concat_axis=1, tiled=T...]
    ppermute x6 -> x0, starting transfers between devices: 7.1 us -> none  [neighbours(): return (lax.ppermute(tail, axis, up), lax.ppermute(head, axis, down))]
    pallas_call x1 -> x0, local copies, waits for them, and re-layouts: 2.03 us -> none  [on_device(): call(lookup_kernel, ((6, PLANE, SLOTS), F32), [], 'lookup')]
    slice x2 -> x0, local copies, waits for them, and re-layouts: 1.92 us -> none  [the longest x1 0.99 us: on_device(): left, right = neighbours(density[:w], density[CX - w:], 'bx')]
  transfers between devices with their start and end apart: 7 -> 0, of which waited for: 5 -> 0; matrix products, arithmetic and copies ran while one was open for 0% -> 0% of each run, Pallas kernels for 3% -> 0%
where the time goes in v2:
time: 130 us
  Pallas kernels  125 us (96%)
  local copies, waits for them, and re-layouts  4.45 us (3%)
    pallas_call x1, Pallas kernels, on_device(): pl.pallas_call(step_kernel, out_shape=[jax.ShapeDtypeStruct(*o) for o in...  125 us
    unnamed x5, local copies, waits for them, and re-layouts  4.45 us

profile of v2, /device:TPU:1, one launch (start us, length us, event | category | flops | bytes accessed | tf_op | source)
XLA Modules:
  0.0 130.0 jit_solution(2317995875129021305)
XLA Ops:
  0.6 124.9 %step.1 = (f32[3,4096]{1,0:T(4,128)}, f32[3,4096]{1,0:T(4,128)}, f32[2,16,64,64]{3,2,1,0:T(8,128)}) custom-call(s32[2,8,4096]{2,1,0:T(8,128)} %slot_ref.1, f32[8,4096]{1,0:T(8,128)} %weight_ref.1, s32[1,4096]{1,0:T(1,128)} %bitcast.1, s32[3,64,256]{2,1,0:T(8,128)} %cell_ref.1, s32[2,3840]{1,0:T(2,128)} %pairs_ref.1, f32[3,4096]{1,0:T(4,128)} %pos_ref.1, ...), custom_call_target="tpu_custom_call" | custom-call | tf_op jit(solution)/shard_map/step/pallas_call | solution.py:572
  125.5 0.0 copy-start
  125.5 1.5 %copy.15 = f32[3,4096]{1,0:T(4,128)} copy(f32[3,4096]{1,0:T(4,128)} %get-tuple-element.6) | data formatting | bytes 98304
  127.1 0.0 copy-done
  127.1 0.6 copy.16
  127.7 2.3 %copy.17 = f32[2,16,64,64]{3,2,1,0:T(8,128)} copy(f32[2,16,64,64]{3,2,1,0:T(8,128)} %get-tuple-element.8) | data formatting | bytes 1048576
Async XLA Ops:
  125.5 1.5 %copy-start = (f32[3,4096]{1,0:T(4,128)S(1)}, f32[3,4096]{1,0:T(4,128)}, u32[]{:S(2)}) copy-start(f32[3,4096]{1,0:T(4,128)} %get-tuple-element.7) | copy-start | bytes 147460

commit v3 on v2

--- a/solution.py
+++ b/solution.py
@@ -21,10 +21,9 @@
 OWNERS = ("bx", "by", "bz")
 N_BY = 8
 MESH = pl.DeviceIdType.MESH
-PACK_CHUNK = 1024
 SPREAD_ROWS = 8
-GATHER_ROWS = 2
-FORCE_CHUNK = 512
+GATHER_ROWS = 4
+FORCE_CHUNK = 1024
 YP = 72
 W = REACH + 1
 WIDE = 2 * CZ
@@ -38,6 +37,7 @@
 
 F32 = jnp.float32
 BF16 = jnp.bfloat16
+F8 = jnp.float8_e4m3fn
 NT = (((1,), (1,)), ((), ()))
 NN = (((1,), (0,)), ((), ()))
 
@@ -64,6 +64,49 @@
     rest = x - hi.astype(F32)
     mid = rest.astype(BF16)
     return hi, mid, (rest - mid.astype(F32)).astype(BF16)
+
+
+PIECES = 3
+SHRINK = 2.0**-4
+
+
+def scales(biggest):
+    power = 7.0 - jnp.ceil(jnp.log2(jnp.maximum(biggest, 1e-30)))
+    return jnp.exp2(power), jnp.exp2(-power)
+
+
+def pieces(x, scale):
+    rest = x * scale
+    out = []
+    for n in range(PIECES):
+        out.append(rest.astype(F8))
+        rest = (rest - out[-1].astype(F32)) * (1.0 / SHRINK)
+    return out
+
+
+def mm_pieces(table_ref, columns):
+    depth = table_ref.shape[1] // PIECES
+    total = mm(table_ref[:, :depth], columns[0])
+    for n in range(1, PIECES):
+        total = total + mm(table_ref[:, n * depth : (n + 1) * depth], columns[n])
+    return total
+
+
+def onehot8(index, rows):
+    mask = lax.broadcasted_iota(jnp.int32, (rows, index.shape[1]), 0).astype(
+        jnp.int8
+    ) == index.astype(jnp.int8)
+    return [
+        jnp.where(mask, jnp.asarray(SHRINK**n, F8), jnp.zeros((), F8)) for n in range(PIECES)
+    ]
+
+
+def onehot8_xy(x, y):
+    oys = onehot8(y, CY)
+    xb = jnp.broadcast_to(x.astype(F32).astype(BF16), oys[0].shape)
+    zero = jnp.zeros((), F8)
+    masks = [xb == jnp.asarray(i, BF16) for i in range(CX)]
+    return [jnp.concatenate([jnp.where(m, oy, zero) for m in masks], axis=0) for oy in oys]
 
 
 def rows_iota(rows, n, dtype=BF16):
@@ -95,14 +138,11 @@
     ]
 
 
-def onehot_xy(x, y):
+def onehot_xy(x, y, planes):
     oy = onehot(y, CY)
     xb = x.astype(F32).astype(BF16)
     zero = jnp.zeros((), BF16)
-    blocks = []
-    for i in range(CX):
-        blocks.append(jnp.where(xb == jnp.asarray(i, BF16), oy, zero))
-    return jnp.concatenate(blocks, axis=0)
+    return jnp.concatenate([jnp.where(xb == jnp.asarray(i, BF16), oy, zero) for i in planes], axis=0)
 
 
 def z_operators():
@@ -142,44 +182,66 @@
 def pack(slot_ref, weight_ref, species_ref, send_ref, acc_ref):
     acc_ref[...] = jnp.zeros_like(acc_ref)
 
-    def body(step, carry):
-        c = step % 8
-        cols = pl.ds(pl.multiple_of((step // 8) * PACK_CHUNK, PACK_CHUNK), PACK_CHUNK)
-        brick = slot_ref[0, pl.ds(c, 1), cols]
-        slot = slot_ref[1, pl.ds(c, 1), cols]
-        kd = brick + PLANE * species_ref[:, cols]
-        hi, lo = two(weight_ref[pl.ds(c, 1), cols])
+    def body(c, carry):
+        brick = slot_ref[0, pl.ds(c, 1), :]
+        slot = slot_ref[1, pl.ds(c, 1), :]
+        kd = brick + PLANE * species_ref[...]
+        hi, lo = two(weight_ref[pl.ds(c, 1), :])
         left = jnp.concatenate([weighted(kd, 2 * PLANE, hi), weighted(kd, 2 * PLANE, lo)], axis=0)
         acc_ref[...] += mm(left, onehot(slot, SLOTS), NT)
         return carry
 
-    lax.fori_loop(0, 8 * BEADS_DEV // PACK_CHUNK, body, 0)
+    lax.fori_loop(0, 8, body, 0)
     total = acc_ref[: 2 * PLANE] + acc_ref[2 * PLANE :]
     send_ref[:, 0, :] = total[:PLANE]
     send_ref[:, 1, :] = total[PLANE:]
 
 
-def spread(me, arrive, recv_ref, cell_ref, ext_ref, xy_ref, z_ref, acc_ref):
-    acc_ref[...] = jnp.zeros_like(acc_ref)
-
-    def body(step, carry):
+EDGE = tuple(range(W)) + tuple(range(CX - W, CX))
+INNER = tuple(range(W, CX - W))
+
+
+def spread(me, arrive, edge_done, recv_ref, cell_ref, ext_ref, xy_ref, z_ref, acc_ref):
+    span = SPREAD_ROWS * SLOTS
+
+    def source(t):
+        return lax.rem(me - t + PLANE, PLANE)
+
+    def put_z(step):
         for i in range(SPREAD_ROWS):
             t = step * SPREAD_ROWS + i
-            p = lax.rem(me - t + PLANE, PLANE)
-            arrive(t, p)
-            x, y, z = (cell_ref[a, pl.ds(p, 1), :] for a in range(3))
+            arrive(t, source(t))
+        for i in range(SPREAD_ROWS):
+            p = source(step * SPREAD_ROWS + i)
+            z = cell_ref[2, pl.ds(p, 1), :]
             cols = slice(i * SLOTS, (i + 1) * SLOTS)
-            xy_ref[:, cols] = onehot_xy(x, y)
             for k in range(2):
                 hi, lo = two(recv_ref[p, k : k + 1, :])
-                z_ref[k * CZ : (k + 1) * CZ, cols] = weighted(z, CZ, hi)
-                z_ref[(2 + k) * CZ : (3 + k) * CZ, cols] = weighted(z, CZ, lo)
-        acc_ref[...] += mm(xy_ref[...], z_ref[...], NT)
-        return carry
-
-    lax.fori_loop(0, PLANE // SPREAD_ROWS, body, 0)
-    total = (acc_ref[:, :WIDE] + acc_ref[:, WIDE:]) * (CX * CY * CZ / BEADS_DEV)
-    ext_ref[W : W + CX] = total.reshape(CX, CY, WIDE)
+                z_ref[step, k * CZ : (k + 1) * CZ, cols] = weighted(z, CZ, hi)
+                z_ref[step, (2 + k) * CZ : (3 + k) * CZ, cols] = weighted(z, CZ, lo)
+
+    def part(planes, with_z):
+        acc_ref[...] = jnp.zeros_like(acc_ref)
+
+        def body(step, carry):
+            if with_z:
+                put_z(step)
+            for i in range(SPREAD_ROWS):
+                p = source(step * SPREAD_ROWS + i)
+                x, y = (cell_ref[a, pl.ds(p, 1), :] for a in range(2))
+                xy_ref[:, i * SLOTS : (i + 1) * SLOTS] = onehot_xy(x, y, planes)
+            acc_ref[...] += mm(xy_ref[...], z_ref[step], NT)
+            return carry
+
+        lax.fori_loop(0, PLANE // SPREAD_ROWS, body, 0)
+        total = (acc_ref[:, :WIDE] + acc_ref[:, WIDE:]) * (CX * CY * CZ / BEADS_DEV)
+        return total.reshape(len(planes), CY, WIDE)
+
+    edge = part(EDGE, True)
+    ext_ref[W : 2 * W] = edge[:W]
+    ext_ref[CX : CX + W] = edge[W:]
+    edge_done()
+    ext_ref[2 * W : CX] = part(INNER, False)
 
 
 def filter_x(ext_ref, ey_ref, head_ref, tail_ref):
@@ -194,7 +256,7 @@
         tail_ref[i] = total[CY - W :]
         return carry
 
-    lax.fori_loop(0, CX + 2, body, 0)
+    lax.fori_loop(0, CX + 2, body, 0, unroll=3)
 
 
 def filter_y(left_ref, right_ref, ey_ref, ay_ref, head_ref, tail_ref):
@@ -219,84 +281,109 @@
         tail_ref[i] = edge[8:]
         return carry
 
-    lax.fori_loop(0, CX + 2, body, 0)
-
-
-def slopes(left_ref, right_ref, op_ref, hop_ref, ay_ref, smooth_ref, table_ref, p_ref, pz_ref):
+    lax.fori_loop(0, CX + 2, body, 0, unroll=3)
+
+
+def slopes(
+    left_ref, right_ref, op_ref, hop_ref, ay_ref, smooth_ref, table_ref, p_ref, pz_ref, slope_ref
+):
     op_hi, op_lo = two(op_ref[...])
     hop_hi, hop_lo = two(hop_ref[...])
 
     def filter_z(i, carry):
         halo = jnp.concatenate([left_ref[i], right_ref[i]], axis=0).T
         both = mm3(ay_ref[i], op_hi, op_lo) + mm3(halo, hop_hi, hop_lo)
+        smooth_ref[i] = both[1 : CY + 1, :WIDE]
         p_ref[i] = both[:, WIDE : 2 * WIDE]
         pz_ref[i] = both[:, 2 * WIDE :]
-
-        @pl.when((i > 0) & (i <= CX))
+        return carry
+
+    lax.fori_loop(0, CX + 2, filter_z, 0, unroll=3)
+
+    biggest = jnp.zeros((CY, WIDE), F32)
+    for q in range(1, CX + 1):
+        sx = (p_ref[q + 1, 1 : CY + 1] - p_ref[q - 1, 1 : CY + 1]) * 0.5
+        sy = (p_ref[q, 2 : CY + 2] - p_ref[q, :CY]) * 0.5
+        sz = pz_ref[q, 1 : CY + 1]
+        for a, slope in enumerate((sx, sy, sz)):
+            slope_ref[a, (q - 1) * CY : q * CY] = slope
+            biggest = jnp.maximum(biggest, jnp.abs(slope))
+    scale, inverse = scales(jnp.max(biggest))
+    for i in range(0, CX * CY, 128):
+        for a in range(3):
+            for n, piece in enumerate(pieces(slope_ref[a, i : i + 128].T, scale)):
+                table_ref[a * WIDE : (a + 1) * WIDE, n * CX * CY + i : n * CX * CY + i + 128] = piece
+    return inverse
+
+
+def lookup(me, leave, table_ref, inverse, cell_ref, send_ref, a, b):
+    def owners(t):
+        return [lax.rem(me + 1 + t * GATHER_ROWS + i + PLANE, PLANE) for i in range(GATHER_ROWS)]
+
+    def place(t, axis):
+        return jnp.concatenate([cell_ref[axis, pl.ds(p, 1), :] for p in owners(t)], axis=1)
+
+    def build(t, refs):
+        for n, columns in enumerate(onehot8_xy(place(t, 0), place(t, 1))):
+            refs[0][n] = columns
+
+    def multiply(refs):
+        refs[1][...] = mm_pieces(table_ref, refs[0][...])
+
+    def choose(t, refs):
+        found = pick(place(t, 2), CZ, refs[1][...])
+        for i, p in enumerate(owners(t)):
+            cols = slice(i * SLOTS, (i + 1) * SLOTS)
+            send_ref[p] = jnp.concatenate([found[g][:, cols] for g in range(6)], axis=0) * inverse
+
+    b[1][...] = jnp.zeros_like(b[1])
+    build(0, a)
+    steps = PLANE // GATHER_ROWS
+
+    def body(s, carry):
+        t = 2 * s
+        multiply(a)
+        build(t + 1, b)
+        choose(t - 1, b)
+        multiply(b)
+        build(t + 2, a)
+        choose(t, a)
+
+        @pl.when(s > 0)
         def _():
-            for k in range(2):
-                smooth_ref[k, i - 1] = both[1 : CY + 1, k * CZ : (k + 1) * CZ]
-
-        return carry
-
-    lax.fori_loop(0, CX + 2, filter_z, 0)
-
-    for i in range(0, CX, 2):
-        parts = []
-        for q in (i + 1, i + 2):
-            sx = (p_ref[q + 1, 1 : CY + 1] - p_ref[q - 1, 1 : CY + 1]) * 0.5
-            sy = (p_ref[q, 2 : CY + 2] - p_ref[q, :CY]) * 0.5
-            sz = pz_ref[q, 1 : CY + 1]
-            parts.append((sx, sy, sz))
-        cols = slice(i * CY, (i + 2) * CY)
-        for a in range(3):
-            hi, lo = two(jnp.concatenate([parts[0][a], parts[1][a]], axis=0).T)
-            table_ref[a * WIDE : (a + 1) * WIDE, cols] = hi
-            table_ref[(3 + a) * WIDE : (4 + a) * WIDE, cols] = lo
-
-
-def lookup(me, leave, table_ref, cell_ref, send_ref):
-    def body(step, carry):
-        owners = [lax.rem(me + 1 + step * GATHER_ROWS + i, PLANE) for i in range(GATHER_ROWS)]
-        xyz = [
-            jnp.concatenate([cell_ref[a, pl.ds(p, 1), :] for p in owners], axis=1)
-            for a in range(3)
-        ]
-        both = mm(table_ref[...], onehot_xy(xyz[0], xyz[1]))
-        half = 6 * CZ
-        found = pick(xyz[2], CZ, both[:half] + both[half:])
-        for i, p in enumerate(owners):
-            cols = slice(i * SLOTS, (i + 1) * SLOTS)
-            send_ref[p] = jnp.concatenate([found[g][:, cols] for g in range(6)], axis=0)
-        for p in owners:
+            for p in owners(t - 1):
+                leave(p)
+
+        for p in owners(t):
             leave(p)
         return carry
 
-    lax.fori_loop(0, PLANE // GATHER_ROWS, body, 0)
-
-
-def forces(
-    recv_ref, slot_ref, weight_ref, species_ref, vel_ref, delta_ref, hi_ref, lo_ref
-):
+    lax.fori_loop(0, steps // 2, body, 0)
+    choose(steps - 1, b)
+    for p in owners(steps - 1)[:-1]:
+        leave(p)
+
+
+def forces(recv_ref, slot_ref, weight_ref, species_ref, vel_ref, delta_ref, table_ref):
     for g in range(6):
-        hi, lo = two(recv_ref[:, g, :])
-        hi_ref[g * PLANE : (g + 1) * PLANE] = hi
-        lo_ref[g * PLANE : (g + 1) * PLANE] = lo
+        for n, part in enumerate(two(recv_ref[:, g, :])):
+            table_ref[(6 * n + g) * PLANE : (6 * n + g + 1) * PLANE] = part
     wide = 2 * PLANE
+    half = 6 * PLANE
 
     def body(step, carry):
         cols = pl.ds(pl.multiple_of(step * FORCE_CHUNK, FORCE_CHUNK), FORCE_CHUNK)
         species = species_ref[:, cols]
         force = [jnp.zeros((1, FORCE_CHUNK), F32)] * 3
         for c in range(8):
-            oh = onehot(slot_ref[1, c : c + 1, cols], SLOTS)
-            both = mm(hi_ref[...], oh) + mm(lo_ref[...], oh)
-            found = pick(slot_ref[0, c : c + 1, cols] + PLANE * species, wide, both)
+            both = mm(table_ref[...], onehot(slot_ref[1, c : c + 1, cols], SLOTS))
+            brick = slot_ref[0, c : c + 1, cols] + PLANE * species
+            found = pick(brick, wide, both[:half] + both[half:])
             weight = weight_ref[c : c + 1, cols]
             force = [force[a] - weight * found[a] for a in range(3)]
         for a in range(3):
-            half = vel_ref[a : a + 1, cols] + 0.5 * time_step * force[a]
-            delta_ref[a : a + 1, cols] = time_step * half
+            half_step = vel_ref[a : a + 1, cols] + 0.5 * time_step * force[a]
+            delta_ref[a : a + 1, cols] = time_step * half_step
         return carry
 
     lax.fori_loop(0, BEADS_DEV // FORCE_CHUNK, body, 0)
@@ -336,6 +423,7 @@
 def constrain(pairs_ref, bonds_ref, delta_ref, pos_ref, newpos_ref, newvel_ref, oh_ref, nb_ref):
     pairs = jnp.concatenate([pairs_ref[0:1], pairs_ref[1:2]], axis=1)
     hi_index = pairs >> 7
+    oh_ref[...] = onehot(pairs & 127, 128)
     r = [bonds_ref[a : a + 1] for a in range(3)]
     other = jnp.concatenate([bonds_ref[3:4], bonds_ref[4:5]], axis=1).astype(jnp.int32)
     sign = [bonds_ref[5:6], bonds_ref[6:7]]
@@ -375,19 +463,18 @@
         newvel_ref[a : a + 1] = change / time_step
 
 
-def step_kernel(
+def field_kernel(
     slot_ref,
     weight_ref,
     species_ref,
     cell_ref,
     pairs_ref,
     pos_ref,
-    vel_ref,
     op_ref,
     hop_ref,
-    newpos_ref,
-    newvel_ref,
+    recv2_ref,
     smooth_ref,
+    bonds_ref,
     acc1_ref,
     send1_ref,
     recv1_ref,
@@ -401,21 +488,22 @@
     zside_ref,
     p_ref,
     pz_ref,
+    s_ref,
+    slope_ref,
     table_ref,
     send2_ref,
-    recv2_ref,
-    hi_ref,
-    lo_ref,
-    delta_ref,
-    bonds_ref,
+    cols_a_ref,
+    found_a_ref,
+    cols_b_ref,
+    found_b_ref,
     oh_ref,
-    nb_ref,
     out_sem,
     in_sem,
     back_out_sem,
     back_in_sem,
     side_out_sem,
     side_in_sem,
+    own_sem,
 ):
     bx, by, bz = (lax.axis_index(a) for a in OWNERS)
     me = bx * N_BY + by
@@ -472,10 +560,8 @@
         def _():
             forward(p, p).wait_recv()
 
-    spread(me, arrive, recv1_ref, cell_ref, ext_ref, xy_ref, z_ref, acc2_ref)
-
-    def exchange(axis, to_left, to_right, from_left, from_right):
-        copies = [
+    def sides(axis, to_left, to_right, from_left, from_right):
+        return [
             pltpu.make_async_remote_copy(
                 src_ref=src,
                 dst_ref=dst,
@@ -488,41 +574,60 @@
                 ((to_left, from_right, -1), (to_right, from_left, 1))
             )
         ]
+
+    def start(copies):
         for copy in copies:
             copy.start()
+
+    def wait(copies):
         for copy in copies:
             copy.wait()
 
-    exchange(
+    along_x = sides(
         0,
         ext_ref.at[pl.ds(W, W)],
         ext_ref.at[pl.ds(CX, W)],
         ext_ref.at[pl.ds(0, W)],
         ext_ref.at[pl.ds(W + CX, W)],
     )
+    along_y = sides(1, *(yside_ref.at[n] for n in range(4)))
+    along_z = sides(2, *(zside_ref.at[n] for n in range(4)))
+    spread(
+        me, arrive, lambda: start(along_x), recv1_ref, cell_ref, ext_ref, xy_ref, z_ref, acc2_ref
+    )
+    wait(along_x)
     filter_x(ext_ref, ey_ref, yside_ref.at[0], yside_ref.at[1])
-    exchange(1, *(yside_ref.at[n] for n in range(4)))
+    start(along_y)
+    wait(along_y)
     filter_y(yside_ref.at[2], yside_ref.at[3], ey_ref, ay_ref, zside_ref.at[0], zside_ref.at[1])
-    exchange(2, *(zside_ref.at[n] for n in range(4)))
-    slopes(
+    start(along_z)
+    wait(along_z)
+    inverse = slopes(
         zside_ref.at[2],
         zside_ref.at[3],
         op_ref,
         hop_ref,
         ay_ref,
-        smooth_ref,
+        s_ref,
         table_ref,
         p_ref,
         pz_ref,
-    )
-
-    def leave(p):
-        @pl.when(p != me)
-        def _():
-            back(p, me).start()
-
-    lookup(me, leave, table_ref, cell_ref, send2_ref)
-    recv2_ref[me] = send2_ref[me]
+        slope_ref,
+    )
+    keep = pltpu.make_async_copy(s_ref.at[pl.ds(1, CX)], smooth_ref, own_sem.at[0])
+    keep.start()
+    lookup(
+        me,
+        lambda p: back(p, me).start(),
+        table_ref,
+        inverse,
+        cell_ref,
+        send2_ref,
+        (cols_a_ref, found_a_ref),
+        (cols_b_ref, found_b_ref),
+    )
+    own = pltpu.make_async_copy(send2_ref.at[me], recv2_ref.at[me], own_sem.at[1])
+    own.start()
 
     def finish(t, carry):
         p = lax.rem(me + t, PLANE)
@@ -533,22 +638,50 @@
         return carry
 
     lax.fori_loop(1, PLANE, finish, 0)
-    forces(
-        recv2_ref, slot_ref, weight_ref, species_ref, vel_ref, delta_ref, hi_ref, lo_ref
-    )
+    own.wait()
+    keep.wait()
+
+
+def bead_kernel(
+    recv_ref,
+    fields_ref,
+    bonds_ref,
+    slot_ref,
+    weight_ref,
+    species_ref,
+    pairs_ref,
+    pos_ref,
+    vel_ref,
+    newpos_ref,
+    newvel_ref,
+    smooth_ref,
+    split_ref,
+    table_ref,
+    delta_ref,
+    oh_ref,
+    nb_ref,
+    sem,
+):
+    for k in range(2):
+        split_ref[k] = fields_ref[:, :, k * CZ : (k + 1) * CZ]
+    keep = pltpu.make_async_copy(split_ref, smooth_ref, sem.at[0])
+    keep.start()
+    forces(recv_ref, slot_ref, weight_ref, species_ref, vel_ref, delta_ref, table_ref)
     constrain(pairs_ref, bonds_ref, delta_ref, pos_ref, newpos_ref, newvel_ref, oh_ref, nb_ref)
+    keep.wait()
 
 
 def on_device(positions, velocities, species, corner_slot, corner_weight, slot_cell, bond_pairs):
     own_op, halo_op = z_operators()
     layers = CX + 2
+    group = GATHER_ROWS * SLOTS
     scratch = [
         ((256, SLOTS), F32),
         ((PLANE, 2, SLOTS), F32),
         ((PLANE, 2, SLOTS), F32),
-        ((CX * CY, SPREAD_ROWS * SLOTS), BF16),
-        ((4 * CZ, SPREAD_ROWS * SLOTS), BF16),
-        ((CX * CY, 4 * CZ), F32),
+        ((CX * CY // 2, SPREAD_ROWS * SLOTS), BF16),
+        ((PLANE // SPREAD_ROWS, 4 * CZ, SPREAD_ROWS * SLOTS), BF16),
+        ((CX * CY // 2, 4 * CZ), F32),
         ((CX + 2 * W, CY, WIDE), F32),
         ((layers, CY + 2 * W, WIDE), F32),
         ((4, layers, W, WIDE), F32),
@@ -556,39 +689,77 @@
         ((4, layers, 8, YP), F32),
         ((layers, YP, WIDE), F32),
         ((layers, YP, WIDE), F32),
-        ((6 * WIDE, CX * CY), BF16),
+        ((layers, CY, WIDE), F32),
+        ((3, CX * CY, WIDE), F32),
+        ((3 * WIDE, PIECES * CX * CY), F8),
         ((PLANE, 6, SLOTS), F32),
-        ((PLANE, 6, SLOTS), F32),
-        ((6 * PLANE, SLOTS), BF16),
-        ((6 * PLANE, SLOTS), BF16),
-        ((3, BEADS_DEV), F32),
-        ((8, BONDS_DEV), F32),
-        ((128, ENDS), BF16),
+        ((PIECES, CX * CY, group), F8),
+        ((3 * WIDE, group), F32),
+        ((PIECES, CX * CY, group), F8),
+        ((3 * WIDE, group), F32),
         ((128, ENDS), BF16),
     ]
     vmem = pl.BlockSpec(memory_space=pltpu.VMEM)
-    outs = [((3, BEADS_DEV), F32), ((3, BEADS_DEV), F32), ((2, CX, CY, CZ), F32)]
+    hbm = pl.BlockSpec(memory_space=pl.ANY)
     dma = pltpu.SemaphoreType.DMA
-    moved, new_velocities, smoothed = pl.pallas_call(
-        step_kernel,
-        out_shape=[jax.ShapeDtypeStruct(*o) for o in outs],
-        in_specs=[vmem] * 9,
-        out_specs=[vmem] * 3,
-        scratch_shapes=[pltpu.VMEM(*s) for s in scratch] + [dma((PLANE,))] * 4 + [dma((6,))] * 2,
+    limit = 60 * 1024 * 1024
+    species = species[None, :]
+    returned, fields, bond_data = pl.pallas_call(
+        field_kernel,
+        out_shape=[
+            jax.ShapeDtypeStruct((PLANE, 6, SLOTS), F32),
+            jax.ShapeDtypeStruct((CX, CY, WIDE), F32),
+            jax.ShapeDtypeStruct((8, BONDS_DEV), F32),
+        ],
+        in_specs=[vmem] * 8,
+        out_specs=[hbm, hbm, vmem],
+        scratch_shapes=[pltpu.VMEM(*s) for s in scratch]
+        + [dma((PLANE,))] * 4
+        + [dma((6,))] * 2
+        + [dma((2,))],
         compiler_params=pltpu.CompilerParams(
-            vmem_limit_bytes=60 * 1024 * 1024, collective_id=0, has_side_effects=True
+            vmem_limit_bytes=limit, collective_id=0, has_side_effects=True
         ),
-        name="step",
+        name="field",
     )(
         corner_slot,
         corner_weight,
-        species[None, :],
+        species,
         slot_cell,
         bond_pairs,
         positions,
-        velocities,
         jnp.asarray(own_op),
         jnp.asarray(halo_op),
+    )
+    moved, new_velocities, smoothed = pl.pallas_call(
+        bead_kernel,
+        out_shape=[
+            jax.ShapeDtypeStruct((3, BEADS_DEV), F32),
+            jax.ShapeDtypeStruct((3, BEADS_DEV), F32),
+            jax.ShapeDtypeStruct((2, CX, CY, CZ), F32),
+        ],
+        in_specs=[vmem] * 9,
+        out_specs=[vmem, vmem, hbm],
+        scratch_shapes=[
+            pltpu.VMEM((2, CX, CY, CZ), F32),
+            pltpu.VMEM((12 * PLANE, SLOTS), BF16),
+            pltpu.VMEM((3, BEADS_DEV), F32),
+            pltpu.VMEM((128, ENDS), BF16),
+            pltpu.VMEM((128, ENDS), BF16),
+            dma((1,)),
+        ],
+        compiler_params=pltpu.CompilerParams(vmem_limit_bytes=limit),
+        name="bead",
+    )(
+        returned,
+        fields,
+        bond_data,
+        corner_slot,
+        corner_weight,
+        species,
+        bond_pairs,
+        positions,
+        velocities,
     )
     return (moved, new_velocities, smoothed)
 

time: 130 us -> 102 us (0.78)
  Pallas kernels: 125 us -> 101 us
  local copies, waits for them, and re-layouts: 4.45 us -> 0 us
    pallas_call x1 -> x2, Pallas kernels: 125 us -> 101 us  [the longest x1 76.9 us: on_device(): pl.pallas_call(field_kernel, out_shape=[jax.ShapeDtypeStruct((PLANE, 6, S...]
    unnamed x5 -> x0, local copies, waits for them, and re-layouts: 4.45 us -> none
where the time goes in v3:
time: 102 us; the launch traced here: 101 us
  Pallas kernels  101 us (99%)
    pallas_call x1, Pallas kernels, on_device(): pl.pallas_call(field_kernel, out_shape=[jax.ShapeDtypeStruct((PLANE, 6, S...  76.9 us
    pallas_call x1, Pallas kernels, on_device(): pl.pallas_call(bead_kernel, out_shape=[jax.ShapeDtypeStruct((3, BEADS_DEV...  23.8 us

profile of v3, /device:TPU:1, one launch (start us, length us, event | category | flops | bytes accessed | tf_op | source)
XLA Modules:
  0.0 101.5 jit_solution(13336369679956985880)
XLA Ops:
  0.6 76.9 %field.1 = (f32[64,6,256]{2,1,0:T(8,128)}, f32[16,64,128]{2,1,0:T(8,128)}, f32[8,3840]{1,0:T(8,128)}) custom-call(s32[2,8,4096]{2,1,0:T(8,128)} %slot_ref.3, f32[8,4096]{1,0:T(8,128)} %weight_ref.3, s32[1,4096]{1,0:T(1,128)} %bitcast.1, s32[3,64,256]{2,1,0:T(8,128)} %cell_ref.1, s32[2,3840]{1,0:T(2,128)} %pairs_ref.3, f32[3,4096]{1,0:T(4,128)} %pos_ref.3, ...), custom_call_target="tpu_custom_call" | custom-call | tf_op jit(solution)/shard_map/field/pallas_call | solution.py:707
  77.5 23.8 %bead.1 = (f32[3,4096]{1,0:T(4,128)}, f32[3,4096]{1,0:T(4,128)}, f32[2,16,64,64]{3,2,1,0:T(8,128)}) custom-call(f32[64,6,256]{2,1,0:T(8,128)} %get-tuple-element.6.recv_ref, f32[16,64,128]{2,1,0:T(8,128)} %get-tuple-element.7.fields_ref, f32[8,3840]{1,0:T(8,128)} %get-tuple-element.8.bonds_ref, s32[2,8,4096]{2,1,0:T(8,128)} %slot_ref.3, ...), custom_call_target="tpu_custom_call" | custom-call | tf_op jit(solution)/shard_map/bead/pallas_call | solution.py:734

commit v4 on v3

--- a/solution.py
+++ b/solution.py
@@ -23,6 +23,7 @@
 MESH = pl.DeviceIdType.MESH
 SPREAD_ROWS = 8
 GATHER_ROWS = 4
+BACK = 8
 FORCE_CHUNK = 1024
 YP = 72
 W = REACH + 1
@@ -68,6 +69,7 @@
 
 PIECES = 3
 SHRINK = 2.0**-4
+WEIGHT_SCALE = 128.0
 
 
 def scales(biggest):
@@ -92,10 +94,13 @@
     return total
 
 
+def same8(index, rows):
+    row = lax.broadcasted_iota(jnp.int32, (rows, index.shape[1]), 0)
+    return row.astype(jnp.int8) == index.astype(jnp.int8)
+
+
 def onehot8(index, rows):
-    mask = lax.broadcasted_iota(jnp.int32, (rows, index.shape[1]), 0).astype(
-        jnp.int8
-    ) == index.astype(jnp.int8)
+    mask = same8(index, rows)
     return [
         jnp.where(mask, jnp.asarray(SHRINK**n, F8), jnp.zeros((), F8)) for n in range(PIECES)
     ]
@@ -185,14 +190,21 @@
     def body(c, carry):
         brick = slot_ref[0, pl.ds(c, 1), :]
         slot = slot_ref[1, pl.ds(c, 1), :]
-        kd = brick + PLANE * species_ref[...]
-        hi, lo = two(weight_ref[pl.ds(c, 1), :])
-        left = jnp.concatenate([weighted(kd, 2 * PLANE, hi), weighted(kd, 2 * PLANE, lo)], axis=0)
-        acc_ref[...] += mm(left, onehot(slot, SLOTS), NT)
+        mask = same8(brick + PLANE * species_ref[...], 2 * PLANE)
+        left = [
+            jnp.where(mask, jnp.broadcast_to(piece, mask.shape), jnp.zeros((), F8))
+            for piece in pieces(weight_ref[pl.ds(c, 1), :], WEIGHT_SCALE)
+        ]
+        right = jnp.where(same8(slot, SLOTS), jnp.ones((), F8), jnp.zeros((), F8))
+        acc_ref[...] += mm(jnp.concatenate(left, axis=0), right, NT)
         return carry
 
     lax.fori_loop(0, 8, body, 0)
-    total = acc_ref[: 2 * PLANE] + acc_ref[2 * PLANE :]
+    rows = 2 * PLANE
+    total = acc_ref[(PIECES - 1) * rows :]
+    for n in range(PIECES - 2, -1, -1):
+        total = acc_ref[n * rows : (n + 1) * rows] + SHRINK * total
+    total = total * (1.0 / WEIGHT_SCALE)
     send_ref[:, 0, :] = total[:PLANE]
     send_ref[:, 1, :] = total[PLANE:]
 
@@ -259,8 +271,27 @@
     lax.fori_loop(0, CX + 2, body, 0, unroll=3)
 
 
-def filter_y(left_ref, right_ref, ey_ref, ay_ref, head_ref, tail_ref):
+def filter_rows(ey_ref, i, first, rows):
     taps = gauss_taps()
+    total = taps[0] * ey_ref[i, first : first + rows]
+    for j in range(1, 2 * REACH + 1):
+        total = total + taps[j] * ey_ref[i, first + j : first + j + rows]
+    return total
+
+
+Y_LOW = 8
+Y_HIGH = 56
+
+
+def filter_y_inner(ey_ref, ay_ref):
+    def body(i, carry):
+        ay_ref[i, Y_LOW:Y_HIGH] = filter_rows(ey_ref, i, Y_LOW, Y_HIGH - Y_LOW)
+        return carry
+
+    lax.fori_loop(0, CX + 2, body, 0, unroll=3)
+
+
+def filter_y_edge(left_ref, right_ref, ey_ref, ay_ref, head_ref, tail_ref):
     span = CY + 2
     row = lax.broadcasted_iota(jnp.int32, (16, WIDE), 0)
     lane = lax.broadcasted_iota(jnp.int32, (16, WIDE), 1)
@@ -268,13 +299,15 @@
     select = jnp.where(lane == wanted, 1.0, 0.0).astype(BF16)
     ey_ref[:, :W] = left_ref[...]
     ey_ref[:, W + CY :] = right_ref[...]
+    blank = jnp.zeros((YP - span, WIDE), F32)
+    pad = jnp.zeros((WIDE - YP, WIDE), F32)
 
     def body(i, carry):
-        total = taps[0] * ey_ref[i, :span]
-        for j in range(1, 2 * REACH + 1):
-            total = total + taps[j] * ey_ref[i, j : j + span]
-        full = jnp.concatenate([total, jnp.zeros((YP - span, WIDE), F32)], axis=0)
-        ay_ref[i] = full
+        low = filter_rows(ey_ref, i, 0, Y_LOW)
+        high = jnp.concatenate([filter_rows(ey_ref, i, Y_HIGH, span - Y_HIGH), blank], axis=0)
+        ay_ref[i, :Y_LOW] = low
+        ay_ref[i, Y_HIGH:] = high
+        full = jnp.concatenate([low, ay_ref[i, Y_LOW:Y_HIGH], high, pad], axis=0)
         hi, mid, lo = three(full)
         edge = mm(select, hi, NT) + mm(select, mid, NT) + mm(select, lo, NT)
         head_ref[i] = edge[:8]
@@ -284,22 +317,30 @@
     lax.fori_loop(0, CX + 2, body, 0, unroll=3)
 
 
+def filter_z_own(op_ref, ay_ref, part_ref):
+    op_hi, op_lo = two(op_ref[...])
+
+    def body(i, carry):
+        part_ref[i] = mm3(ay_ref[i], op_hi, op_lo)
+        return carry
+
+    lax.fori_loop(0, CX + 2, body, 0, unroll=3)
+
+
 def slopes(
-    left_ref, right_ref, op_ref, hop_ref, ay_ref, smooth_ref, table_ref, p_ref, pz_ref, slope_ref
+    left_ref, right_ref, hop_ref, part_ref, smooth_ref, table_ref, p_ref, pz_ref, slope_ref
 ):
-    op_hi, op_lo = two(op_ref[...])
     hop_hi, hop_lo = two(hop_ref[...])
 
     def filter_z(i, carry):
         halo = jnp.concatenate([left_ref[i], right_ref[i]], axis=0).T
-        both = mm3(ay_ref[i], op_hi, op_lo) + mm3(halo, hop_hi, hop_lo)
+        both = part_ref[i] + mm3(halo[:YP], hop_hi, hop_lo)
         smooth_ref[i] = both[1 : CY + 1, :WIDE]
         p_ref[i] = both[:, WIDE : 2 * WIDE]
         pz_ref[i] = both[:, 2 * WIDE :]
         return carry
 
     lax.fori_loop(0, CX + 2, filter_z, 0, unroll=3)
-
     biggest = jnp.zeros((CY, WIDE), F32)
     for q in range(1, CX + 1):
         sx = (p_ref[q + 1, 1 : CY + 1] - p_ref[q - 1, 1 : CY + 1]) * 0.5
@@ -334,7 +375,10 @@
         found = pick(place(t, 2), CZ, refs[1][...])
         for i, p in enumerate(owners(t)):
             cols = slice(i * SLOTS, (i + 1) * SLOTS)
-            send_ref[p] = jnp.concatenate([found[g][:, cols] for g in range(6)], axis=0) * inverse
+            blank = jnp.zeros((BACK - 6, SLOTS), F32)
+            send_ref[p] = (
+                jnp.concatenate([found[g][:, cols] for g in range(6)] + [blank], axis=0) * inverse
+            )
 
     b[1][...] = jnp.zeros_like(b[1])
     build(0, a)
@@ -365,25 +409,26 @@
 
 
 def forces(recv_ref, slot_ref, weight_ref, species_ref, vel_ref, delta_ref, table_ref):
+    received = recv_ref[...]
+    scale, inverse = scales(jnp.max(jnp.max(jnp.abs(received), axis=0)))
+    table = pltpu.einshape("dgs->gds", received)
     for g in range(6):
-        for n, part in enumerate(two(recv_ref[:, g, :])):
-            table_ref[(6 * n + g) * PLANE : (6 * n + g + 1) * PLANE] = part
+        for n, piece in enumerate(pieces(table[g], scale)):
+            table_ref[g * PLANE : (g + 1) * PLANE, n * SLOTS : (n + 1) * SLOTS] = piece
     wide = 2 * PLANE
-    half = 6 * PLANE
 
     def body(step, carry):
         cols = pl.ds(pl.multiple_of(step * FORCE_CHUNK, FORCE_CHUNK), FORCE_CHUNK)
         species = species_ref[:, cols]
         force = [jnp.zeros((1, FORCE_CHUNK), F32)] * 3
         for c in range(8):
-            both = mm(table_ref[...], onehot(slot_ref[1, c : c + 1, cols], SLOTS))
-            brick = slot_ref[0, c : c + 1, cols] + PLANE * species
-            found = pick(brick, wide, both[:half] + both[half:])
+            both = mm_pieces(table_ref, onehot8(slot_ref[1, c : c + 1, cols], SLOTS))
+            found = pick(slot_ref[0, c : c + 1, cols] + PLANE * species, wide, both)
             weight = weight_ref[c : c + 1, cols]
             force = [force[a] - weight * found[a] for a in range(3)]
         for a in range(3):
-            half_step = vel_ref[a : a + 1, cols] + 0.5 * time_step * force[a]
-            delta_ref[a : a + 1, cols] = time_step * half_step
+            half = vel_ref[a : a + 1, cols] + (0.5 * time_step) * (force[a] * inverse)
+            delta_ref[a : a + 1, cols] = time_step * half
         return carry
 
     lax.fori_loop(0, BEADS_DEV // FORCE_CHUNK, body, 0)
@@ -486,6 +531,7 @@
     yside_ref,
     ay_ref,
     zside_ref,
+    part_ref,
     p_ref,
     pz_ref,
     s_ref,
@@ -598,16 +644,19 @@
     wait(along_x)
     filter_x(ext_ref, ey_ref, yside_ref.at[0], yside_ref.at[1])
     start(along_y)
+    filter_y_inner(ey_ref, ay_ref)
     wait(along_y)
-    filter_y(yside_ref.at[2], yside_ref.at[3], ey_ref, ay_ref, zside_ref.at[0], zside_ref.at[1])
+    filter_y_edge(
+        yside_ref.at[2], yside_ref.at[3], ey_ref, ay_ref, zside_ref.at[0], zside_ref.at[1]
+    )
     start(along_z)
+    filter_z_own(op_ref, ay_ref, part_ref)
     wait(along_z)
     inverse = slopes(
         zside_ref.at[2],
         zside_ref.at[3],
-        op_ref,
         hop_ref,
-        ay_ref,
+        part_ref,
         s_ref,
         table_ref,
         p_ref,
@@ -676,7 +725,7 @@
     layers = CX + 2
     group = GATHER_ROWS * SLOTS
     scratch = [
-        ((256, SLOTS), F32),
+        ((PIECES * 2 * PLANE, SLOTS), F32),
         ((PLANE, 2, SLOTS), F32),
         ((PLANE, 2, SLOTS), F32),
         ((CX * CY // 2, SPREAD_ROWS * SLOTS), BF16),
@@ -686,13 +735,14 @@
         ((layers, CY + 2 * W, WIDE), F32),
         ((4, layers, W, WIDE), F32),
         ((layers, YP, WIDE), F32),
-        ((4, layers, 8, YP), F32),
+        ((4, layers, 8, WIDE), F32),
+        ((layers, YP, 3 * WIDE), F32),
         ((layers, YP, WIDE), F32),
         ((layers, YP, WIDE), F32),
         ((layers, CY, WIDE), F32),
         ((3, CX * CY, WIDE), F32),
         ((3 * WIDE, PIECES * CX * CY), F8),
-        ((PLANE, 6, SLOTS), F32),
+        ((PLANE, BACK, SLOTS), F32),
         ((PIECES, CX * CY, group), F8),
         ((3 * WIDE, group), F32),
         ((PIECES, CX * CY, group), F8),
@@ -702,12 +752,12 @@
     vmem = pl.BlockSpec(memory_space=pltpu.VMEM)
     hbm = pl.BlockSpec(memory_space=pl.ANY)
     dma = pltpu.SemaphoreType.DMA
-    limit = 60 * 1024 * 1024
+    limit = 40 * 1024 * 1024
     species = species[None, :]
     returned, fields, bond_data = pl.pallas_call(
         field_kernel,
         out_shape=[
-            jax.ShapeDtypeStruct((PLANE, 6, SLOTS), F32),
+            jax.ShapeDtypeStruct((PLANE, BACK, SLOTS), F32),
             jax.ShapeDtypeStruct((CX, CY, WIDE), F32),
             jax.ShapeDtypeStruct((8, BONDS_DEV), F32),
         ],
@@ -742,7 +792,7 @@
         out_specs=[vmem, vmem, hbm],
         scratch_shapes=[
             pltpu.VMEM((2, CX, CY, CZ), F32),
-            pltpu.VMEM((12 * PLANE, SLOTS), BF16),
+            pltpu.VMEM((6 * PLANE, PIECES * SLOTS), F8),
             pltpu.VMEM((3, BEADS_DEV), F32),
             pltpu.VMEM((128, ENDS), BF16),
             pltpu.VMEM((128, ENDS), BF16),

time: 102 us -> 101 us (level)
  Pallas kernels: 101 us -> 92.8 us
  local copies, waits for them, and re-layouts: 0 us -> 6.75 us
    unnamed x0 -> x18, local copies, waits for them, and re-layouts: none -> 6.75 us
    pallas_call x1, Pallas kernels: 76.9 us -> 72.5 us  [on_device(): pl.pallas_call(field_kernel, out_shape=[jax.ShapeDtypeStruct((PLANE, BACK...]
    pallas_call x1, Pallas kernels: 23.8 us -> 20.3 us  [on_device(): pl.pallas_call(bead_kernel, out_shape=[jax.ShapeDtypeStruct((3, BEADS_DEV...]
where the time goes in v4:
time: 101 us; the launch traced here: 100 us
  Pallas kernels  92.8 us (92%)
  local copies, waits for them, and re-layouts  6.75 us (7%)
    pallas_call x1, Pallas kernels, on_device(): pl.pallas_call(field_kernel, out_shape=[jax.ShapeDtypeStruct((PLANE, BACK...  72.5 us
    pallas_call x1, Pallas kernels, on_device(): pl.pallas_call(bead_kernel, out_shape=[jax.ShapeDtypeStruct((3, BEADS_DEV...  20.3 us
    unnamed x18, local copies, waits for them, and re-layouts  6.75 us

profile of v4, /device:TPU:1, one launch (start us, length us, event | category | flops | bytes accessed | tf_op | source)
XLA Modules:
  0.0 100.4 jit_solution(1327916905293320093)
XLA Ops:
  0.6 0.0 copy-start
  0.6 0.9 copy-done
  1.6 0.0 copy-start.1
  1.6 0.9 copy-done.1
  2.5 0.0 copy-start.2
  2.5 0.8 copy-done.2
  3.3 0.0 copy-start.3
  3.3 0.9 copy-done.3
  4.3 0.0 copy-start.4
  4.3 0.9 copy-done.4
  5.2 0.0 copy-start.5
  5.2 0.8 copy-done.5
  5.9 0.0 copy-start.6
  5.9 0.7 copy-done.6
  6.7 0.0 copy-start.8
  6.7 0.7 copy-done.8
  7.4 0.0 copy-start.7
  7.4 72.5 %field.1 = (f32[64,8,256]{2,1,0:T(8,128)S(1)}, f32[16,64,128]{2,1,0:T(8,128)S(1)}, f32[8,3840]{1,0:T(8,128)S(1)}) custom-call(s32[2,8,4096]{2,1,0:T(8,128)S(1)} %copy-done, f32[8,4096]{1,0:T(8,128)S(1)} %copy-done.1, s32[1,4096]{1,0:T(1,128)S(1)} %bitcast.1, s32[3,64,256]{2,1,0:T(8,128)S(1)} %copy-done.3, s32[2,3840]{1,0:T(2,128)S(1)} %copy-done.5, ...), custom_call_target="tpu_custom_call" | custom-call | tf_op jit(solution)/shard_map/field/pallas_call | solution.py:757
  79.9 0.0 copy-done.7
  79.9 20.3 %bead.1 = (f32[3,4096]{1,0:T(4,128)}, f32[3,4096]{1,0:T(4,128)}, f32[2,16,64,64]{3,2,1,0:T(8,128)}) custom-call(f32[64,8,256]{2,1,0:T(8,128)S(1)} %get-tuple-element.6.recv_ref, f32[16,64,128]{2,1,0:T(8,128)S(1)} %get-tuple-element.7.fields_ref, f32[8,3840]{1,0:T(8,128)S(1)} %get-tuple-element.8.bonds_ref, s32[2,8,4096]{2,1,0:T(8,128)S(1)} %copy-done, ...), custom_call_target="tpu_custom_call" | custom-call | tf_op jit(solution)/shard_map/bead/pallas_call | solution.py:784
Async XLA Ops:
  0.6 1.0 copy-start
  1.6 0.9 copy-start.1
  2.5 0.8 copy-start.2
  3.3 0.9 copy-start.3
  4.3 0.9 copy-start.4
  5.2 0.8 copy-start.5
  5.9 0.7 copy-start.6
  6.7 0.7 copy-start.8
  7.4 72.5 %copy-start.7 = (f32[3,4096]{1,0:T(4,128)S(1)}, f32[3,4096]{1,0:T(4,128)}, u32[]{:S(2)}) copy-start(f32[3,4096]{1,0:T(4,128)} %vel_ref.1) | copy-start | bytes 147460

commit v5 on v4

--- a/solution.py
+++ b/solution.py
@@ -24,6 +24,7 @@
 SPREAD_ROWS = 8
 GATHER_ROWS = 4
 BACK = 8
+LAYERS = 6
 FORCE_CHUNK = 1024
 YP = 72
 W = REACH + 1
@@ -293,10 +294,6 @@
 
 def filter_y_edge(left_ref, right_ref, ey_ref, ay_ref, head_ref, tail_ref):
     span = CY + 2
-    row = lax.broadcasted_iota(jnp.int32, (16, WIDE), 0)
-    lane = lax.broadcasted_iota(jnp.int32, (16, WIDE), 1)
-    wanted = ((row % 8) // W) * CZ + (row // 8) * (CZ - W) + row % W
-    select = jnp.where(lane == wanted, 1.0, 0.0).astype(BF16)
     ey_ref[:, :W] = left_ref[...]
     ey_ref[:, W + CY :] = right_ref[...]
     blank = jnp.zeros((YP - span, WIDE), F32)
@@ -307,11 +304,9 @@
         high = jnp.concatenate([filter_rows(ey_ref, i, Y_HIGH, span - Y_HIGH), blank], axis=0)
         ay_ref[i, :Y_LOW] = low
         ay_ref[i, Y_HIGH:] = high
-        full = jnp.concatenate([low, ay_ref[i, Y_LOW:Y_HIGH], high, pad], axis=0)
-        hi, mid, lo = three(full)
-        edge = mm(select, hi, NT) + mm(select, mid, NT) + mm(select, lo, NT)
-        head_ref[i] = edge[:8]
-        tail_ref[i] = edge[8:]
+        full = jnp.concatenate([low, ay_ref[i, Y_LOW:Y_HIGH], high, pad], axis=0).T
+        head_ref[i] = jnp.concatenate([full[:W], full[CZ : CZ + W]], axis=0)
+        tail_ref[i] = jnp.concatenate([full[CZ - W : CZ], full[WIDE - W :]], axis=0)
         return carry
 
     lax.fori_loop(0, CX + 2, body, 0, unroll=3)
@@ -319,12 +314,11 @@
 
 def filter_z_own(op_ref, ay_ref, part_ref):
     op_hi, op_lo = two(op_ref[...])
-
-    def body(i, carry):
-        part_ref[i] = mm3(ay_ref[i], op_hi, op_lo)
-        return carry
-
-    lax.fori_loop(0, CX + 2, body, 0, unroll=3)
+    twice = jnp.concatenate([op_hi, op_hi], axis=0)
+    for i in range(0, CX + 2, LAYERS):
+        hi, lo = two(ay_ref[i : i + LAYERS].reshape(LAYERS * YP, WIDE))
+        own = mm(jnp.concatenate([hi, lo], axis=1), twice) + mm(hi, op_lo)
+        part_ref[i : i + LAYERS] = own.reshape(LAYERS, YP, 3 * WIDE)
 
 
 def slopes(
@@ -332,15 +326,16 @@
 ):
     hop_hi, hop_lo = two(hop_ref[...])
 
-    def filter_z(i, carry):
-        halo = jnp.concatenate([left_ref[i], right_ref[i]], axis=0).T
-        both = part_ref[i] + mm3(halo[:YP], hop_hi, hop_lo)
-        smooth_ref[i] = both[1 : CY + 1, :WIDE]
-        p_ref[i] = both[:, WIDE : 2 * WIDE]
-        pz_ref[i] = both[:, 2 * WIDE :]
-        return carry
-
-    lax.fori_loop(0, CX + 2, filter_z, 0, unroll=3)
+    for i in range(0, CX + 2, LAYERS):
+        halo = [
+            jnp.concatenate([left_ref[q], right_ref[q]], axis=0).T[:YP]
+            for q in range(i, i + LAYERS)
+        ]
+        both = mm3(jnp.concatenate(halo, axis=0), hop_hi, hop_lo)
+        both = part_ref[i : i + LAYERS] + both.reshape(LAYERS, YP, 3 * WIDE)
+        smooth_ref[i : i + LAYERS] = both[:, 1 : CY + 1, :WIDE]
+        p_ref[i : i + LAYERS] = both[:, :, WIDE : 2 * WIDE]
+        pz_ref[i : i + LAYERS] = both[:, :, 2 * WIDE :]
     biggest = jnp.zeros((CY, WIDE), F32)
     for q in range(1, CX + 1):
         sx = (p_ref[q + 1, 1 : CY + 1] - p_ref[q - 1, 1 : CY + 1]) * 0.5
@@ -465,19 +460,24 @@
     out_ref[7:8] = jnp.zeros((1, HALF), F32)
 
 
+def put_twice(ref, columns):
+    ref[:128] = columns
+    ref[128:] = columns
+
+
 def constrain(pairs_ref, bonds_ref, delta_ref, pos_ref, newpos_ref, newvel_ref, oh_ref, nb_ref):
     pairs = jnp.concatenate([pairs_ref[0:1], pairs_ref[1:2]], axis=1)
     hi_index = pairs >> 7
-    oh_ref[...] = onehot(pairs & 127, 128)
+    put_twice(oh_ref, onehot(pairs & 127, 128))
     r = [bonds_ref[a : a + 1] for a in range(3)]
     other = jnp.concatenate([bonds_ref[3:4], bonds_ref[4:5]], axis=1).astype(jnp.int32)
     sign = [bonds_ref[5:6], bonds_ref[6:7]]
     other_hi = other >> 7
-    nb_ref[...] = onehot(other & 127, 128)
+    put_twice(nb_ref, onehot(other & 127, 128))
     delta = [delta_ref[a : a + 1] for a in range(3)]
     parts = [two(to_rows(d)) for d in delta]
     table = [jnp.concatenate([parts[a][q] for a in range(3)], axis=0) for q in range(2)]
-    ends = pick(hi_index, 32, mm(table[0], oh_ref[...]) + mm(table[1], oh_ref[...]))
+    ends = pick(hi_index, 32, mm(jnp.concatenate(table, axis=1), oh_ref[...]))
     v = [r[a] + (ends[a][:, :HALF] - ends[a][:, HALF:]) for a in range(3)]
     total = [jnp.zeros((1, HALF), F32)] * 3
     for sweep in range(SWEEPS):
@@ -491,7 +491,7 @@
         pad = jnp.zeros((2, 128), F32)
         parts = [two(jnp.concatenate([to_rows(s), pad], axis=0)) for s in shift]
         table = [jnp.concatenate([parts[a][q] for a in range(3)], axis=0) for q in range(2)]
-        near = pick(other_hi, 32, mm(table[0], nb_ref[...]) + mm(table[1], nb_ref[...]))
+        near = pick(other_hi, 32, mm(jnp.concatenate(table, axis=1), nb_ref[...]))
         v = [
             v[a] - 2.0 * shift[a] - sign[0] * near[a][:, :HALF] + sign[1] * near[a][:, HALF:]
             for a in range(3)
@@ -500,7 +500,7 @@
     for a in range(3):
         both = jnp.concatenate([total[a], -total[a]], axis=1)
         rows += [weighted(hi_index, 32, q) for q in two(both)]
-    moved = mm(jnp.concatenate(rows, axis=0), oh_ref[...], NT)
+    moved = mm(jnp.concatenate(rows, axis=0), oh_ref[:128], NT)
     for a in range(3):
         q = to_line(moved[64 * a : 64 * a + 32] + moved[64 * a + 32 : 64 * a + 64])
         change = delta[a] - q
@@ -509,14 +509,14 @@
 
 
 def field_kernel(
-    slot_ref,
-    weight_ref,
-    species_ref,
-    cell_ref,
-    pairs_ref,
-    pos_ref,
-    op_ref,
-    hop_ref,
+    slot_hbm,
+    weight_hbm,
+    species_hbm,
+    cell_hbm,
+    pairs_hbm,
+    pos_hbm,
+    op_hbm,
+    hop_hbm,
     recv2_ref,
     smooth_ref,
     bonds_ref,
@@ -543,6 +543,14 @@
     cols_b_ref,
     found_b_ref,
     oh_ref,
+    slot_ref,
+    weight_ref,
+    species_ref,
+    cell_ref,
+    pairs_ref,
+    pos_ref,
+    op_ref,
+    hop_ref,
     out_sem,
     in_sem,
     back_out_sem,
@@ -550,7 +558,25 @@
     side_out_sem,
     side_in_sem,
     own_sem,
+    input_sem,
 ):
+    inputs = [
+        pltpu.make_async_copy(src, dst, input_sem.at[n])
+        for n, (src, dst) in enumerate(
+            (
+                (slot_hbm, slot_ref),
+                (weight_hbm, weight_ref),
+                (species_hbm, species_ref),
+                (pairs_hbm, pairs_ref),
+                (pos_hbm, pos_ref),
+                (cell_hbm, cell_ref),
+                (op_hbm, op_ref),
+                (hop_hbm, hop_ref),
+            )
+        )
+    ]
+    for copy in inputs:
+        copy.start()
     bx, by, bz = (lax.axis_index(a) for a in OWNERS)
     me = bx * N_BY + by
     counts = [lax.axis_size(a) for a in OWNERS]
@@ -574,6 +600,8 @@
     for by_how in (-1, 1):
         pl.semaphore_signal(barrier, inc=1, device_id=shifted(2, by_how), device_id_type=MESH)
 
+    for copy in inputs[:3]:
+        copy.wait()
     pack(slot_ref, weight_ref, species_ref, send1_ref, acc1_ref)
     pl.semaphore_wait(barrier, PLANE + 1)
 
@@ -599,6 +627,8 @@
 
     lax.fori_loop(1, PLANE, send, 0)
     recv1_ref[me] = send1_ref[me]
+    for copy in inputs[3:]:
+        copy.wait()
     bonds(pairs_ref, pos_ref, bonds_ref, oh_ref)
 
     def arrive(t, p):
@@ -722,6 +752,7 @@
 
 def on_device(positions, velocities, species, corner_slot, corner_weight, slot_cell, bond_pairs):
     own_op, halo_op = z_operators()
+    species = species[None, :]
     layers = CX + 2
     group = GATHER_ROWS * SLOTS
     scratch = [
@@ -749,11 +780,23 @@
         ((3 * WIDE, group), F32),
         ((128, ENDS), BF16),
     ]
+    scratch += [
+        (a.shape, a.dtype)
+        for a in (
+            corner_slot,
+            corner_weight,
+            species,
+            slot_cell,
+            bond_pairs,
+            positions,
+            own_op,
+            halo_op,
+        )
+    ]
     vmem = pl.BlockSpec(memory_space=pltpu.VMEM)
     hbm = pl.BlockSpec(memory_space=pl.ANY)
     dma = pltpu.SemaphoreType.DMA
-    limit = 40 * 1024 * 1024
-    species = species[None, :]
+    limit = 60 * 1024 * 1024
     returned, fields, bond_data = pl.pallas_call(
         field_kernel,
         out_shape=[
@@ -761,12 +804,12 @@
             jax.ShapeDtypeStruct((CX, CY, WIDE), F32),
             jax.ShapeDtypeStruct((8, BONDS_DEV), F32),
         ],
-        in_specs=[vmem] * 8,
+        in_specs=[pl.BlockSpec(memory_space=pltpu.HBM)] * 8,
         out_specs=[hbm, hbm, vmem],
         scratch_shapes=[pltpu.VMEM(*s) for s in scratch]
         + [dma((PLANE,))] * 4
         + [dma((6,))] * 2
-        + [dma((2,))],
+        + [dma((2,)), dma((8,))],
         compiler_params=pltpu.CompilerParams(
             vmem_limit_bytes=limit, collective_id=0, has_side_effects=True
         ),
@@ -794,8 +837,8 @@
             pltpu.VMEM((2, CX, CY, CZ), F32),
             pltpu.VMEM((6 * PLANE, PIECES * SLOTS), F8),
             pltpu.VMEM((3, BEADS_DEV), F32),
-            pltpu.VMEM((128, ENDS), BF16),
-            pltpu.VMEM((128, ENDS), BF16),
+            pltpu.VMEM((256, ENDS), BF16),
+            pltpu.VMEM((256, ENDS), BF16),
             dma((1,)),
         ],
         compiler_params=pltpu.CompilerParams(vmem_limit_bytes=limit),

time: 101 us -> 93.3 us (0.924)
  local copies, waits for them, and re-layouts: 6.75 us -> 0 us
    unnamed x18 -> x0, local copies, waits for them, and re-layouts: 6.75 us -> none
where the time goes in v5:
time: 93.3 us; the launch traced here: 93.2 us
  Pallas kernels  92.4 us (99%)
    pallas_call x1, Pallas kernels, on_device(): pl.pallas_call(field_kernel, out_shape=[jax.ShapeDtypeStruct((PLANE, BACK...  71.6 us
    pallas_call x1, Pallas kernels, on_device(): pl.pallas_call(bead_kernel, out_shape=[jax.ShapeDtypeStruct((3, BEADS_DEV...  20.8 us

profile of v5, /device:TPU:1, one launch (start us, length us, event | category | flops | bytes accessed | tf_op | source)
XLA Modules:
  0.0 93.2 jit_solution(12088480371371354842)
XLA Ops:
  0.6 71.6 %field.1 = (f32[64,8,256]{2,1,0:T(8,128)}, f32[16,64,128]{2,1,0:T(8,128)}, f32[8,3840]{1,0:T(8,128)}) custom-call(s32[2,8,4096]{2,1,0:T(8,128)} %slot_ref.1, f32[8,4096]{1,0:T(8,128)} %weight_ref.1, s32[1,4096]{1,0:T(1,128)} %bitcast.1, s32[3,64,256]{2,1,0:T(8,128)} %cell_hbm.1, s32[2,3840]{1,0:T(2,128)} %pairs_ref.1, f32[3,4096]{1,0:T(4,128)} %pos_ref.1, ...), custom_call_target="tpu_custom_call" | custom-call | tf_op jit(solution)/shard_map/field/pallas_call | solution.py:800
  72.2 20.8 %bead.1 = (f32[3,4096]{1,0:T(4,128)}, f32[3,4096]{1,0:T(4,128)}, f32[2,16,64,64]{3,2,1,0:T(8,128)}) custom-call(f32[64,8,256]{2,1,0:T(8,128)} %get-tuple-element.6.recv_ref, f32[16,64,128]{2,1,0:T(8,128)} %get-tuple-element.7.fields_ref, f32[8,3840]{1,0:T(8,128)} %get-tuple-element.8.bonds_ref, s32[2,8,4096]{2,1,0:T(8,128)} %slot_ref.1, ...), custom_call_target="tpu_custom_call" | custom-call | tf_op jit(solution)/shard_map/bead/pallas_call | solution.py:827

commit v6 on v5

--- a/solution.py
+++ b/solution.py
@@ -21,7 +21,7 @@
 OWNERS = ("bx", "by", "bz")
 N_BY = 8
 MESH = pl.DeviceIdType.MESH
-SPREAD_ROWS = 8
+SPREAD_ROWS = 32
 GATHER_ROWS = 4
 BACK = 8
 LAYERS = 6
@@ -188,7 +188,7 @@
 def pack(slot_ref, weight_ref, species_ref, send_ref, acc_ref):
     acc_ref[...] = jnp.zeros_like(acc_ref)
 
-    def body(c, carry):
+    def part(c):
         brick = slot_ref[0, pl.ds(c, 1), :]
         slot = slot_ref[1, pl.ds(c, 1), :]
         mask = same8(brick + PLANE * species_ref[...], 2 * PLANE)
@@ -197,10 +197,13 @@
             for piece in pieces(weight_ref[pl.ds(c, 1), :], WEIGHT_SCALE)
         ]
         right = jnp.where(same8(slot, SLOTS), jnp.ones((), F8), jnp.zeros((), F8))
-        acc_ref[...] += mm(jnp.concatenate(left, axis=0), right, NT)
+        return mm(jnp.concatenate(left, axis=0), right, NT)
+
+    def body(step, carry):
+        acc_ref[...] += part(2 * step) + part(2 * step + 1)
         return carry
 
-    lax.fori_loop(0, 8, body, 0)
+    lax.fori_loop(0, 4, body, 0)
     rows = 2 * PLANE
     total = acc_ref[(PIECES - 1) * rows :]
     for n in range(PIECES - 2, -1, -1):

time: 93.3 us -> 93 us (level)
  no operation moved by 1% of the time
where the time goes in v6:
time: 93 us; the launch traced here: 92.9 us
  Pallas kernels  92.1 us (99%)
    pallas_call x1, Pallas kernels, on_device(): pl.pallas_call(field_kernel, out_shape=[jax.ShapeDtypeStruct((PLANE, BACK...  71.5 us
    pallas_call x1, Pallas kernels, on_device(): pl.pallas_call(bead_kernel, out_shape=[jax.ShapeDtypeStruct((3, BEADS_DEV...  20.6 us

profile of v6, /device:TPU:1, one launch (start us, length us, event | category | flops | bytes accessed | tf_op | source)
XLA Modules:
  0.0 92.9 jit_solution(705387632868498984)
XLA Ops:
  0.6 71.5 %field.1 = (f32[64,8,256]{2,1,0:T(8,128)}, f32[16,64,128]{2,1,0:T(8,128)}, f32[8,3840]{1,0:T(8,128)}) custom-call(s32[2,8,4096]{2,1,0:T(8,128)} %slot_ref.1, f32[8,4096]{1,0:T(8,128)} %weight_ref.1, s32[1,4096]{1,0:T(1,128)} %bitcast.1, s32[3,64,256]{2,1,0:T(8,128)} %cell_hbm.1, s32[2,3840]{1,0:T(2,128)} %pairs_ref.1, f32[3,4096]{1,0:T(4,128)} %pos_ref.1, ...), custom_call_target="tpu_custom_call" | custom-call | tf_op jit(solution)/shard_map/field/pallas_call | solution.py:803
  72.1 20.6 %bead.1 = (f32[3,4096]{1,0:T(4,128)}, f32[3,4096]{1,0:T(4,128)}, f32[2,16,64,64]{3,2,1,0:T(8,128)}) custom-call(f32[64,8,256]{2,1,0:T(8,128)} %get-tuple-element.6.recv_ref, f32[16,64,128]{2,1,0:T(8,128)} %get-tuple-element.7.fields_ref, f32[8,3840]{1,0:T(8,128)} %get-tuple-element.8.bonds_ref, s32[2,8,4096]{2,1,0:T(8,128)} %slot_ref.1, ...), custom_call_target="tpu_custom_call" | custom-call | tf_op jit(solution)/shard_map/bead/pallas_call | solution.py:830
